TPU v7x, 128 devices: a whole 4x4x4 slice. The times are simulated.
128 devices in a mesh: dp: 32 (over x, z, core), rep: 4 (over y).
Axes of the slice: x: 4, y: 4, z: 4, core: 2. Of those that a mesh axis runs over, the one named last changes fastest.
Arguments:
- events: bfloat16 [65536, 512], P(('dp', 'rep')), may hold values from -6 to 6
- grad_out: bfloat16 [65536, 512], P(('dp', 'rep')), may hold values from -15 to 15
- w_uvqk: bfloat16 [512, 2048], replicated, may hold values from -0.25 to 0.25
- w_out: bfloat16 [512, 512], replicated, may hold values from -0.25 to 0.25
- send_place: int32 [128, 512], P(('dp', 'rep')), may hold values from 0 to 1023, as said below
- send_counts: int32 [128, 32], P(('dp', 'rep')), may hold values from 0 to 32, as said below
- user_ids: int32 [128, 512], P(('dp', 'rep')), may hold values from 0 to 15, never falling along the last dimension, each value on 1 to 256 neighbouring positions
Outputs:
- grad_events: bfloat16 [65536, 512], P(('dp', 'rep'))
- grad_w_uvqk: float32 [512, 2048], P(None, 'dp')
- grad_w_out: float32 [512, 512], P(None, 'dp')
Inputs may be any that keep to these rules, and one draw needn't show every extreme that they name: `send_counts`: row d * 4 + r gives, for each owner o of group r, how many events device (d, r) sends there; each row sums to 512, and the counts one owner receives from the 32 devices of its group also sum to 512. `send_place`: an event bound for owner o has place o * 32 + j, where j runs from 0 to that owner's count minus 1 over the device's events bound for o; each place at most once on a device. `user_ids`: each row lists an owner's users in the owner's order of events; ids never fall.
All inputs are finite; a program needn't handle non-finite values.
Results may differ from a plain program's by a relative error of at most 0.02.
Values may be sent and summed in bfloat16 or wider, within the bound.
A program may use at most 192 MiB of HBM per device.

v0:
```python
import jax
import jax.numpy as jnp
from jax import lax
from jax.sharding import PartitionSpec as P

HEADS = 8


EPSILON = 1e-05


def normalized_row_block(values):
    center = values - jnp.mean(values, axis=-1, keepdims=True)
    spread = jnp.mean(center * center, axis=-1, keepdims=True)
    return center * lax.rsqrt(spread + EPSILON)


def hstu_layer(event_row_block, input_weight_matrix, weight_out, allowed):
    width = weight_out.shape[0]
    count = event_row_block.shape[0]
    head_size = width // HEADS
    normalized_input = normalized_row_block(event_row_block.astype(jnp.float32)).astype(
        jnp.bfloat16
    )
    activation_value = jax.nn.silu(
        jnp.dot(normalized_input, input_weight_matrix, preferred_element_type=jnp.float32)
    ).astype(jnp.bfloat16)
    gate_u = activation_value[:, :width]
    values = activation_value[:, width : 2 * width].reshape(count, HEADS, head_size)
    queries = activation_value[:, 2 * width : 3 * width].reshape(count, HEADS, head_size)
    keys = activation_value[:, 3 * width :].reshape(count, HEADS, head_size)
    scores = jnp.einsum(
        "qhd,khd->hqk", queries, keys, preferred_element_type=jnp.float32
    ) * head_size ** (-0.5)
    weights = (jax.nn.silu(scores) * allowed[None]).astype(jnp.bfloat16)
    attended = jnp.einsum(
        "hqk,khd->qhd", weights, values, preferred_element_type=jnp.float32
    ).reshape(count, width)
    gated = (normalized_row_block(attended) * gate_u.astype(jnp.float32)).astype(jnp.bfloat16)
    return event_row_block.astype(jnp.float32) + jnp.dot(
        gated, weight_out, preferred_element_type=jnp.float32
    )


def owner_grads(event_row_block, cotangent, input_weight_matrix, weight_out, allowed):
    result, pullback = jax.vjp(
        lambda first, second, third: hstu_layer(first, second, third, allowed),
        event_row_block,
        input_weight_matrix,
        weight_out,
    )
    return pullback(cotangent.astype(jnp.float32))


def on_device(events, grad_out, w_uvqk, w_out, send_place, send_counts, user_ids):
    owners = lax.axis_size("dp")
    owned = events.shape[0]
    width = events.shape[1]
    capacity = 2 * owned // owners
    places_out = send_place[0]
    send_rows = jnp.zeros((owners * capacity, width), jnp.bfloat16).at[places_out].set(events)
    send_grads = jnp.zeros((owners * capacity, width), jnp.bfloat16).at[places_out].set(grad_out)
    recv_rows, recv_grads = (
        lax.all_to_all(send_rows, "dp", split_axis=0, concat_axis=0, tiled=True),
        lax.all_to_all(send_grads, "dp", split_axis=0, concat_axis=0, tiled=True),
    )
    count_table = lax.all_gather(send_counts, "dp", axis=0, tiled=True)
    own_index = lax.axis_index("dp")
    counts_in = lax.dynamic_slice_in_dim(count_table, own_index, 1, 1)[:, 0]
    users = user_ids[0]
    target_positions = jnp.arange(owners * capacity, dtype=jnp.int32)
    source = target_positions // capacity
    within = target_positions - source * capacity
    starts = jnp.cumsum(counts_in) - counts_in
    onehot = (jnp.arange(owners, dtype=jnp.int32)[None, :] == source[:, None]).astype(jnp.int32)
    count_at = jnp.sum(onehot * counts_in[None, :], axis=1)
    starting_offset = jnp.sum(onehot * starts[None, :], axis=1)
    valid = within < count_at
    position = jnp.minimum(starting_offset + within, owned - 1)
    slot_users = jnp.take(users, position)
    allowed = (
        valid[:, None]
        & valid[None, :]
        & (slot_users[:, None] == slot_users[None, :])
        & (target_positions[None, :] <= target_positions[:, None])
    ).astype(jnp.float32)
    grad_rows, grad_in, grad_outw = owner_grads(recv_rows, recv_grads, w_uvqk, w_out, allowed)
    returned = lax.all_to_all(grad_rows, "dp", split_axis=0, concat_axis=0, tiled=True)
    grad_events = jnp.take(returned, places_out, axis=0)
    grad_in = grad_in.astype(jnp.float32)
    grad_outw = grad_outw.astype(jnp.float32)
    part_in, part_out = (
        lax.psum_scatter(
            grad_in.astype(jnp.bfloat16), "dp", scatter_dimension=1, tiled=True
        ).astype(jnp.float32),
        lax.psum_scatter(
            grad_outw.astype(jnp.bfloat16), "dp", scatter_dimension=1, tiled=True
        ).astype(jnp.float32),
    )
    share_in, share_out = (
        lax.psum(part_in.astype(jnp.bfloat16), "rep").astype(jnp.float32),
        lax.psum(part_out.astype(jnp.bfloat16), "rep").astype(jnp.float32),
    )
    return (grad_events, share_in, share_out)


def solution(mesh):
    return jax.shard_map(
        on_device,
        mesh=mesh,
        in_specs=(
            P(("dp", "rep"), None),
            P(("dp", "rep"), None),
            P(),
            P(),
            P(("dp", "rep"), None),
            P(("dp", "rep"), None),
            P(("dp", "rep"), None),
        ),
        out_specs=(P(("dp", "rep"), None), P(None, "dp"), P(None, "dp")),
        check_vma=False,
    )
```

profile of v0, /device:TPU:0, one launch (start us, length us, event | category | flops | bytes accessed | tf_op | source)
XLA Modules:
  0.0 388.2 jit_solution(12523036387752850072)
XLA Ops:
  7.2 0.0 copy-start
  7.2 0.8 compare_select_fusion.1
  8.0 4.0 %scatter_custom_fusion.1 = bf16[1024,512]{1,0:T(8,128)(2,1)} fusion(s32[512]{0:T(512)S(1)} %bitcast.106, bf16[512,512]{1,0:T(8,128)(2,1)} %param.7, bf16[]{:T(256)} %constant.83.clone.1), kind=kCustom, calls=%fused_computation.50 | custom fusion | bytes 1049088 | tf_op jit(solution)/shard_map/scatter | solution.py:61
  12.0 8.3 %all-to-all-start.1 = ((bf16[32,32,512]{2,1,0:T(8,128)(2,1)}), bf16[32,32,512]{2,1,0:T(8,128)(2,1)S(1)}, u32[]{:S(2)}, u32[]{:S(2)}) async-start(bf16[32,32,512]{2,1,0:T(8,128)(2,1)} %bitcast.95), calls=%async_computation.1 | async-start | bytes 2097152 | tf_op jit(solution)/shard_map/all_to_all | solution.py:64
  20.3 29.8 %all-gather = s32[32,1,32]{2,1,0:T(1,128)S(1)} all-gather(s32[1,1,32]{2,1,0:T(1,128)} %bitcast.110), channel_id=1, replica_groups=mesh['dp'=32,'rep'=4] {'dp'}, dimensions={0}, use_global_device_ids=true | all-gather | bytes 4224 | tf_op jit(solution)/shard_map/all_gather | solution.py:67
  50.1 0.7 fusion.27
  50.8 0.1 reduce-window.8
  50.9 0.1 reduce.6
  51.0 0.1 select_reduce_fusion.1
  51.1 4.0 %scatter_custom_fusion = bf16[1024,512]{1,0:T(8,128)(2,1)} fusion(s32[512]{0:T(512)S(1)} %bitcast.107, bf16[512,512]{1,0:T(8,128)(2,1)} %param.8, bf16[]{:T(256)} %constant.83.clone.1), kind=kCustom, calls=%fused_computation.52 | custom fusion | bytes 1049088 | tf_op jit(solution)/shard_map/scatter | solution.py:62
  55.1 6.9 %gather_fusion = s32[1024]{0:T(1024)S(1)} fusion(s32[512]{0:T(512)S(1)} %bitcast.87, s32[1024]{0:T(1024)S(1)} %broadcast_clamp_fusion), kind=kCustom, calls=%fused_computation | custom fusion | bytes 12288 | tf_op jit(solution)/shard_map/jit(_take)/gather | solution.py:80
  62.0 2.9 fusion.6
  65.0 0.0 all-to-all-done.1
  65.0 6.0 %all-to-all-start = ((bf16[32,32,512]{2,1,0:T(8,128)(2,1)}), bf16[32,32,512]{2,1,0:T(8,128)(2,1)}, u32[]{:S(2)}, u32[]{:S(2)}) async-start(bf16[32,32,512]{2,1,0:T(8,128)(2,1)} %bitcast.96), calls=%async_computation | async-start | bytes 2097152 | tf_op jit(solution)/shard_map/all_to_all | solution.py:65
  70.9 0.3 reduce-scatter.5.cloned.1.call-start
  71.3 0.2 convert_reduce_fusion
  71.5 0.1 div.65
  71.6 0.5 multiply_reduce_fusion.1
  72.1 0.1 add.153
  72.2 0.3 multiply_convert_fusion.2
  72.5 0.0 copy-done
  72.6 0.0 copy-start.11
  72.6 5.7 %multiply_convert_fusion.1 = (bf16[1024,2048]{0,1:T(8,128)(2,1)S(1)}, f32[1024,2048]{0,1:T(8,128)}) fusion(bf16[1024,512]{1,0:T(8,128)(2,1)S(1)} %multiply_convert_fusion.2, bf16[512,2048]{1,0:T(8,128)(2,1)S(1)} %copy-done), kind=kOutput, calls=%fused_computation.15 | convolution fusion | flops 2157969408 | bytes 15728640 | tf_op jit(solution)/shard_map/jvp()/dot_general | solution.py:26
  78.3 0.0 copy-done.17
  78.3 0.0 copy-done.11
  78.3 1.9 copy-done.5
  80.2 1.8 fusion.28
  82.0 21.5 %multiply_convert_fusion = (bf16[8,1024,1024]{2,1,0:T(8,128)(2,1)}, f32[8,1024,1024]{2,1,0:T(8,128)}) fusion(f32[1024,1024]{1,0:T(8,128)} %fusion.6, bf16[1024,8,64]{0,2,1:T(8,128)(2,1)S(1)} %bitcast.90, bf16[1024,8,64]{0,2,1:T(8,128)(2,1)} %bitcast.101), kind=kOutput, calls=%fused_computation.8 | convolution fusion | flops 1132462080 | bytes 56623104 | tf_op jit(solution)/shard_map/jvp(qhd,khd->hqk)/dot_general | solution.py:32
  103.5 0.0 copy-start.14
  103.5 12.7 %fusion.29 = (f32[1024]{0:T(1024)S(1)}, f32[8,64,1024]{2,1,0:T(8,128)}) fusion(bf16[1024,8,64]{0,2,1:T(8,128)(2,1)} %bitcast.98, bf16[8,1024,1024]{2,1,0:T(8,128)(2,1)} %get-tuple-element.17), kind=kOutput, calls=%fused_computation.96 | convolution fusion | flops 1074265088 | bytes 19927040 | tf_op jit(solution)/shard_map/jvp(hqk,khd->qhd)/dot_general | solution.py:36
  116.1 1.8 fusion.11
  118.0 0.0 all-to-all-done
  118.0 3.2 multiply_reduce_fusion
  121.2 4.4 %fusion.8 = (bf16[1024,512]{0,1:T(8,128)(2,1)S(1)}, f32[1024]{0:T(1024)S(1)}, bf16[1024,512]{0,1:T(8,128)(2,1)}) fusion(f32[8,64,1024]{2,1,0:T(8,128)} %get-tuple-element.20, f32[1024]{0:T(1024)S(1)} %broadcast_multiply_fusion.1, f32[1024]{0:T(1024)S(1)} %get-tuple-element.14, bf16[1024,2048]{0,1:T(8,128)(2,1)} %copy-done.5, f32[1024]{0:T(1024)S(1)} %get-tuple-element.13, ...), kind=kLoop, calls=%fused_computation.29 | loop fusion | flops 7339008 | bytes 6307840 | tf_op jit(solution)/shard_map/jvp()/convert_element_type | solution.py:39
  125.6 2.6 broadcast_add_fusion
  128.1 0.0 copy-done.2
  128.2 4.0 %fusion.33 = bf16[8,64,1024]{2,1,0:T(8,128)(2,1)} fusion(bf16[8,64,1024]{2,1,0:T(8,128)(2,1)S(1)} %bitcast.93, bf16[8,1024,1024]{2,1,0:T(8,128)(2,1)S(1)} %copy-done.2), kind=kOutput, calls=%fused_computation.100 | convolution fusion | flops 1073741824 | bytes 18874368 | tf_op jit(solution)/shard_map/transpose(jvp(hqk,khd->qhd))/dot_general | solution.py:36
  132.2 23.7 %fusion.2 = bf16[8,1024,1024]{2,1,0:T(8,128)(2,1)} fusion(f32[8,1024,1024]{2,1,0:T(8,128)} %get-tuple-element.18, f32[1024,1024]{1,0:T(8,128)S(1)} %copy-done.8, bf16[8,64,1024]{2,1,0:T(8,128)(2,1)S(1)} %bitcast.94, bf16[1024,8,64]{0,2,1:T(8,128)(2,1)S(1)} %bitcast.99), kind=kOutput, calls=%fused_computation.7 | convolution fusion | flops 1191182336 | bytes 56623104 | tf_op jit(solution)/shard_map/transpose(jvp(hqk,khd->qhd))/dot_general | solution.py:36
  155.9 9.8 %fusion.31 = bf16[8,1024,64]{1,2,0:T(8,128)(2,1)} fusion(bf16[8,1024,1024]{2,1,0:T(8,128)(2,1)} %fusion.2, bf16[1024,8,64]{0,2,1:T(8,128)(2,1)S(1)} %bitcast.102), kind=kOutput, calls=%fused_computation.98 | convolution fusion | flops 1073741824 | bytes 18874368 | tf_op jit(solution)/shard_map/transpose(jvp(qhd,khd->hqk))/dot_general | solution.py:32
  165.8 7.5 %fusion.32 = bf16[8,1024,64]{1,2,0:T(8,128)(2,1)S(1)} fusion(bf16[8,1024,1024]{2,1,0:T(8,128)(2,1)} %fusion.2, bf16[1024,8,64]{0,2,1:T(8,128)(2,1)S(1)} %bitcast.91), kind=kOutput, calls=%fused_computation.99 | convolution fusion | flops 1073741824 | bytes 18874368 | tf_op jit(solution)/shard_map/transpose(jvp(qhd,khd->hqk))/dot_general | solution.py:32
  173.2 2.8 convolution_convert_fusion.6
  176.0 0.0 reduce-scatter.5.cloned.1.call-update
  176.1 0.0 reduce-scatter.3.cloned.1.call-start
  176.1 6.4 %fusion.3 = bf16[1024,2048]{0,1:T(8,128)(2,1)S(1)} fusion(f32[1024,2048]{0,1:T(8,128)} %get-tuple-element.16, bf16[1024,512]{0,1:T(8,128)(2,1)} %get-tuple-element.12, bf16[1024,512]{0,1:T(8,128)(2,1)} %bitcast.92, bf16[1024,512]{0,1:T(8,128)(2,1)} %bitcast.100, bf16[1024,512]{0,1:T(8,128)(2,1)S(1)} %bitcast.89), kind=kLoop, calls=%fused_computation.13 | loop fusion | flops 37748736 | bytes 16777216 | tf_op jit(solution)/shard_map/transpose(jvp(jit(silu)))/add_any | solution.py:25
  182.5 1.9 copy-done.9
  184.4 3.7 fusion.30
  188.1 0.0 reduce-scatter.3.cloned.1.call-update
  188.2 0.0 copy-start.20
  188.2 4.9 %fusion.9 = (f32[1024]{0:T(1024)S(1)}, bf16[1024,512]{1,0:T(8,128)(2,1)S(1)}) fusion(bf16[32,32,512]{2,1,0:T(8,128)(2,1)S(1)} %copy-done.4, f32[1024]{0:T(1024)S(1)} %copy-done.16, bf16[1024,2048]{0,1:T(8,128)(2,1)} %copy-done.9, bf16[512,2048]{1,0:T(8,128)(2,1)S(1)} %copy-done), kind=kOutput, calls=%fused_computation.30 | convolution fusion | flops 2150104064 | bytes 8396800 | tf_op jit(solution)/shard_map/transpose(jvp())/dot_general | solution.py:26
  193.1 0.0 copy-start.23
  193.1 1.0 fusion.12
  194.2 2.8 fusion.13
  197.0 7.3 %all-to-all-start.2 = ((bf16[32,32,512]{2,1,0:T(8,128)(2,1)}), bf16[32,32,512]{2,1,0:T(8,128)(2,1)S(1)}, u32[]{:S(2)}, u32[]{:S(2)}) async-start(bf16[32,32,512]{2,1,0:T(8,128)(2,1)} %bitcast.97), calls=%async_computation.2 | async-start | bytes 2097152 | tf_op jit(solution)/shard_map/all_to_all | solution.py:88
  204.3 0.0 all-reduce.6.cloned.1.call-start
  204.4 50.9 %reduce-scatter.5.cloned.1.call-done = bf16[512,16]{0,1:T(8,128)(2,1)} async-done(((bf16[512,512]{0,1:T(8,128)(2,1)}), bf16[512,16]{0,1:T(8,128)(2,1)}) %reduce-scatter.5.cloned.1.call-update) | async-done | bytes 16400 | tf_op jit(solution)/shard_map/reduce_scatter | solution.py:96
  255.3 17.5 %psum.15 = bf16[512,16]{0,1:T(8,128)(2,1)S(1)} all-reduce(bf16[512,16]{0,1:T(8,128)(2,1)} %reduce-scatter.5.cloned.1.call-done), channel_id=1, replica_groups=mesh['dp'=32,'rep'=4] {'rep'}, use_global_device_ids=true, to_apply=%region_16.17 | all-reduce | flops 8192 | bytes 32768 | tf_op jit(solution)/shard_map/psum | solution.py:102
  272.8 0.6 convert_element_type.127
  273.4 0.0 all-to-all-done.2
  273.4 2.6 gather_fusion.1
  276.0 61.1 %reduce-scatter.3.cloned.1.call-done = bf16[512,64]{0,1:T(8,128)(2,1)} async-done(((bf16[512,2048]{0,1:T(8,128)(2,1)}), bf16[512,64]{0,1:T(8,128)(2,1)}) %reduce-scatter.3.cloned.1.call-update) | async-done | bytes 65552 | tf_op jit(solution)/shard_map/reduce_scatter | solution.py:93
  337.2 0.0 all-reduce.6.cloned.1.call-update
  337.2 2.0 broadcast_select_fusion
  339.2 40.8 %all-reduce.6.cloned.1.call-done = bf16[512,64]{0,1:T(8,128)(2,1)} async-done(((bf16[512,64]{0,1:T(8,128)(2,1)}), bf16[512,64]{0,1:T(8,128)(2,1)}) %all-reduce.6.cloned.1.call-update) | async-done | bytes 65552 | tf_op jit(solution)/shard_map/psum | solution.py:101
  379.9 1.5 convert_element_type.124
  (53 shorter events, 0.2 us)
Async XLA Ops:
  7.2 65.4 %copy-start = (bf16[512,2048]{1,0:T(8,128)(2,1)S(1)}, bf16[512,2048]{1,0:T(8,128)(2,1)}, u32[]{:S(2)}) copy-start(bf16[512,2048]{1,0:T(8,128)(2,1)} %param.9) | copy-start | bytes 6291460
  7.2 47.9 %copy-start.1 = (s32[1,512]{1,0:T(1,128)S(1)}, s32[1,512]{1,0:T(1,128)}, u32[]{:S(2)}) copy-start(s32[1,512]{1,0:T(1,128)} %param.13) | copy-start | bytes 6148
  8.0 54.0 %copy-start.21 = (s32[512,1]{0,1:T(1,128)}, s32[512,1]{0,1:T(1,128)S(1)}, u32[]{:S(2)}) copy-start(s32[512,1]{0,1:T(1,128)S(1)} %compare_select_fusion.1) | copy-start | bytes 6148
  12.0 53.0 %all-to-all-start.1 = ((bf16[32,32,512]{2,1,0:T(8,128)(2,1)}), bf16[32,32,512]{2,1,0:T(8,128)(2,1)S(1)}, u32[]{:S(2)}, u32[]{:S(2)}) async-start(bf16[32,32,512]{2,1,0:T(8,128)(2,1)} %bitcast.95), calls=%async_computation.1 | async-start | bytes 2097152 | tf_op jit(solution)/shard_map/all_to_all | solution.py:64
  65.0 13.3 %copy-start.3 = (bf16[32,32,512]{2,1,0:T(8,128)(2,1)}, bf16[32,32,512]{2,1,0:T(8,128)(2,1)S(1)}, u32[]{:S(2)}) copy-start(bf16[32,32,512]{2,1,0:T(8,128)(2,1)S(1)} %all-to-all-done.1) | copy-start | bytes 3145732
  65.0 53.0 %all-to-all-start = ((bf16[32,32,512]{2,1,0:T(8,128)(2,1)}), bf16[32,32,512]{2,1,0:T(8,128)(2,1)}, u32[]{:S(2)}, u32[]{:S(2)}) async-start(bf16[32,32,512]{2,1,0:T(8,128)(2,1)} %bitcast.96), calls=%async_computation | async-start | bytes 2097152 | tf_op jit(solution)/shard_map/all_to_all | solution.py:65
  70.9 184.3 %reduce-scatter.5.cloned.1.call-start = ((), (), s32[]{:S(2)}) async-start(), calls=%async_computation.7 | async-start | bytes 540672 | tf_op jit(solution)/shard_map/reduce_scatter | solution.py:96
  71.6 6.7 %copy-start.15 = (f32[1024]{0:T(1024)}, f32[1024]{0:T(1024)S(1)}, u32[]{:S(2)}) copy-start(f32[1024]{0:T(1024)S(1)} %div.65) | copy-start | bytes 12292
  72.2 6.1 %copy-start.19 = (f32[1024]{0:T(1024)}, f32[1024]{0:T(1024)S(1)}, u32[]{:S(2)}) copy-start(f32[1024]{0:T(1024)S(1)} %add.153) | copy-start | bytes 12292
  72.2 6.1 %copy-start.17 = (f32[1024]{0:T(1024)}, f32[1024]{0:T(1024)S(1)}, u32[]{:S(2)}) copy-start(f32[1024]{0:T(1024)S(1)} %rsqrt.20) | copy-start | bytes 12292
  72.6 5.7 %copy-start.11 = (bf16[1024,512]{1,0:T(8,128)(2,1)}, bf16[1024,512]{1,0:T(8,128)(2,1)S(1)}, u32[]{:S(2)}) copy-start(bf16[1024,512]{1,0:T(8,128)(2,1)S(1)} %multiply_convert_fusion.2) | copy-start | bytes 3145732
  78.3 1.9 copy-start.5
  82.0 21.5 %copy-start.6 = (bf16[1024,512]{0,1:T(8,128)(2,1)}, bf16[1024,512]{0,1:T(8,128)(2,1)S(1)}, u32[]{:S(2)}) copy-start(bf16[1024,512]{0,1:T(8,128)(2,1)S(1)} %get-tuple-element.10) | copy-start | bytes 3145732
  103.5 14.5 %copy-start.14 = (bf16[512,512]{1,0:T(8,128)(2,1)S(1)}, bf16[512,512]{1,0:T(8,128)(2,1)}, u32[]{:S(2)}) copy-start(bf16[512,512]{1,0:T(8,128)(2,1)} %param.10) | copy-start | bytes 1572868
  118.0 10.1 %copy-start.2 = (bf16[8,1024,1024]{2,1,0:T(8,128)(2,1)S(1)}, bf16[8,1024,1024]{2,1,0:T(8,128)(2,1)}, u32[]{:S(2)}) copy-start(bf16[8,1024,1024]{2,1,0:T(8,128)(2,1)} %get-tuple-element.17) | copy-start | bytes 50331652
  128.1 4.0 %copy-start.8 = (f32[1024,1024]{1,0:T(8,128)S(1)}, f32[1024,1024]{1,0:T(8,128)}, u32[]{:S(2)}) copy-start(f32[1024,1024]{1,0:T(8,128)} %fusion.6) | copy-start | bytes 12582916
  128.2 4.0 %copy-start.10 = (bf16[1024,512]{0,1:T(8,128)(2,1)S(1)}, bf16[1024,512]{0,1:T(8,128)(2,1)}, u32[]{:S(2)}) copy-start(bf16[1024,512]{0,1:T(8,128)(2,1)} %get-tuple-element.11) | copy-start | bytes 3145732
  132.2 23.7 %copy-start.13 = (bf16[1024,512]{0,1:T(8,128)(2,1)S(1)}, bf16[1024,512]{0,1:T(8,128)(2,1)}, u32[]{:S(2)}) copy-start(bf16[1024,512]{0,1:T(8,128)(2,1)} %get-tuple-element.9) | copy-start | bytes 3145732
  155.9 9.9 %copy-start.7 = (bf16[1024,512]{0,1:T(8,128)(2,1)S(1)}, bf16[1024,512]{0,1:T(8,128)(2,1)}, u32[]{:S(2)}) copy-start(bf16[1024,512]{0,1:T(8,128)(2,1)} %copy-done.6) | copy-start | bytes 3145732
  176.1 161.1 %reduce-scatter.3.cloned.1.call-start = ((), (), s32[]{:S(2)}) async-start(), calls=%async_computation.5 | async-start | bytes 2162688 | tf_op jit(solution)/shard_map/reduce_scatter | solution.py:93
  176.1 8.3 %copy-start.12 = (bf16[1024,512]{1,0:T(8,128)(2,1)S(1)}, bf16[1024,512]{1,0:T(8,128)(2,1)}, u32[]{:S(2)}) copy-start(bf16[1024,512]{1,0:T(8,128)(2,1)} %copy-done.11) | copy-start | bytes 3145732
  182.5 1.9 copy-start.9
  184.4 3.7 copy-start.4
  184.4 3.7 copy-start.16
  188.2 4.9 %copy-start.20 = (f32[1024]{0:T(1024)S(1)}, f32[1024]{0:T(1024)}, u32[]{:S(2)}) copy-start(f32[1024]{0:T(1024)} %copy-done.19) | copy-start | bytes 12292
  188.2 4.9 %copy-start.18 = (f32[1024]{0:T(1024)S(1)}, f32[1024]{0:T(1024)}, u32[]{:S(2)}) copy-start(f32[1024]{0:T(1024)} %copy-done.17) | copy-start | bytes 12292
  193.1 11.3 %copy-start.22 = (s32[512,1]{0,1:T(1,128)S(1)}, s32[512,1]{0,1:T(1,128)}, u32[]{:S(2)}) copy-start(s32[512,1]{0,1:T(1,128)} %copy-done.21) | copy-start | bytes 6148
  193.1 11.3 %copy-start.23 = (s32[1,512]{1,0:T(1,128)S(1)}, s32[1,512]{1,0:T(1,128)}, u32[]{:S(2)}) copy-start(s32[1,512]{1,0:T(1,128)} %param.11) | copy-start | bytes 6148
  197.0 76.4 %all-to-all-start.2 = ((bf16[32,32,512]{2,1,0:T(8,128)(2,1)}), bf16[32,32,512]{2,1,0:T(8,128)(2,1)S(1)}, u32[]{:S(2)}, u32[]{:S(2)}) async-start(bf16[32,32,512]{2,1,0:T(8,128)(2,1)} %bitcast.97), calls=%async_computation.2 | async-start | bytes 2097152 | tf_op jit(solution)/shard_map/all_to_all | solution.py:88
  204.3 175.6 %all-reduce.6.cloned.1.call-start = ((), (), s32[]{:S(2)}) async-start(), calls=%async_computation.6 | async-start | bytes 131072 | tf_op jit(solution)/shard_map/psum | solution.py:101
Sparse Core Ops, SparseCore 0:
  176.2 79.0 reduce-scatter.4
  258.8 78.2 reduce-scatter.2
  339.5 40.4 all-reduce.5
where the time goes:
time: 395 us; the launch traced here: 388 us
  waiting for transfers between devices  153 us (39%)
  matrix products  99.4 us (25%)
  blocking collectives  47.3 us (12%)
  other arithmetic  28.3 us (7%)
  local copies, waits for them, and re-layouts  24 us (6%)
  starting transfers between devices  22 us (6%)
  between operations  14.4 us (4%)
    reduce_scatter x1, waiting for transfers between devices, on_device(): lax.psum_scatter(grad_in.astype(jnp.bfloat16), 'dp', scatter_dimension=1,...  61.1 us
    reduce_scatter x1, waiting for transfers between devices, on_device(): lax.psum_scatter(grad_outw.astype(jnp.bfloat16), 'dp', scatter_dimension=...  50.9 us
    psum x1, waiting for transfers between devices, on_device(): lax.psum(part_in.astype(jnp.bfloat16), 'rep').astype(jnp.float32)  40.8 us
    dot_general x3, matrix products, hstu_layer(): jnp.einsum('hqk,khd->qhd', weights, values, preferred_element_type=jnp.fl...  40.4 us
    dot_general x3, matrix products, hstu_layer(): jnp.einsum('qhd,khd->hqk', queries, keys, preferred_element_type=jnp.floa...  38.8 us
    all_gather x1, blocking collectives, on_device(): count_table = lax.all_gather(send_counts, 'dp', axis=0, tiled=True)  29.8 us
    psum x1, blocking collectives, on_device(): lax.psum(part_out.astype(jnp.bfloat16), 'rep').astype(jnp.float32)  17.5 us
    dot_general x3, matrix products, hstu_layer(): jnp.dot(normalized_input, input_weight_matrix, preferred_element_type=jnp...  14.3 us
  transfers between devices with their start and end apart: 6, of which 3 were waited for; matrix products, arithmetic and copies ran while one was open for 22% of the time, Pallas kernels for 0%

commit v1 on v0

v1 whole, which is shorter than its diff:
```python
import jax
import jax.numpy as jnp
from jax import lax
from jax.experimental import pallas as pl
from jax.experimental.pallas import tpu as pltpu
from jax.sharding import PartitionSpec as P

HEADS = 8
EPSILON = 1e-05
F32 = jnp.float32
BF16 = jnp.bfloat16
I32 = jnp.int32
MESH = pl.DeviceIdType.MESH
N = 512
DP = 32
REP = 4
CAP = 32
SLOTS = 1024
CHIPS = 16
VMEM_LIMIT = 62 * 1024 * 1024


def dot(a, b):
    return jnp.dot(a, b, preferred_element_type=F32)


def dot_nt(a, b):
    return lax.dot_general(a, b, (((1,), (1,)), ((), ())), preferred_element_type=F32)


def iota(shape, dim):
    return lax.broadcasted_iota(I32, shape, dim)


def onehot(mask):
    return jnp.where(mask, 1.0, 0.0).astype(BF16)


def column_of(row, width):
    return jnp.transpose(jnp.broadcast_to(row, (128, width)))


def position():
    me = lax.axis_index("dp")
    return me, lax.axis_index("rep")


def remote(src, dst, send, recv, dp, rep):
    return pltpu.make_async_remote_copy(
        src_ref=src,
        dst_ref=dst,
        send_sem=send,
        recv_sem=recv,
        device_id=(dp, rep),
        device_id_type=MESH,
    )


def group_signal(barrier, me, rep):
    @pl.loop(1, DP)
    def _(i):
        peer = lax.rem(me + i, DP)
        pl.semaphore_signal(barrier, 1, device_id=(peer, rep), device_id_type=MESH)


def pack(place_ref, rows_ref, out_ref):
    place = place_ref[...]
    for chunk in range(4):
        hot = onehot(iota((256, N), 0) + 256 * chunk == place)
        out_ref[8 * chunk : 8 * chunk + 8] = (
            dot(hot, rows_ref[...]).astype(BF16).reshape(8, CAP, N)
        )


def send_blocks(src, dst, send, recv, local, me, rep):
    @pl.loop(1, DP)
    def _(i):
        peer = lax.rem(me + i, DP)
        remote(src.at[peer], dst.at[me], send.at[peer], recv.at[me], peer, rep).start()

    pltpu.make_async_copy(src.at[me], dst.at[me], local).start()


def wait_blocks(src, dst, send, recv, local, me, rep):
    @pl.loop(1, DP)
    def _(i):
        peer = lax.rem(me + i, DP)
        remote(src.at[peer], dst.at[peer], send.at[peer], recv.at[peer], peer, rep).wait()

    pltpu.make_async_copy(src.at[me], dst.at[me], local).wait()


def send_counts_row(src, dst, send, recv, local, me, rep):
    @pl.loop(1, DP)
    def _(i):
        peer = lax.rem(me + i, DP)
        remote(src, dst.at[me], send.at[peer], recv.at[me], peer, rep).start()

    pltpu.make_async_copy(src, dst.at[me], local).start()


def wait_counts_row(src, dst, send, recv, local, me, rep):
    @pl.loop(1, DP)
    def _(i):
        peer = lax.rem(me + i, DP)
        remote(src, dst.at[peer], send.at[peer], recv.at[peer], peer, rep).wait()

    pltpu.make_async_copy(src, dst.at[me], local).wait()


def dispatch_kernel(
    ev, go, place, cnt, rx, ry, ct, sx, sy, xs, xr, ys, yr, cs, cr, loc
):
    me, rep = position()
    barrier = pltpu.get_barrier_semaphore()
    group_signal(barrier, me, rep)
    pack(place, ev, sx)
    pl.semaphore_wait(barrier, DP - 1)
    send_counts_row(cnt, ct, cs, cr, loc.at[0], me, rep)
    send_blocks(sx, rx, xs, xr, loc.at[1], me, rep)
    pack(place, go, sy)
    send_blocks(sy, ry, ys, yr, loc.at[2], me, rep)
    wait_counts_row(cnt, ct, cs, cr, loc.at[0], me, rep)
    wait_blocks(sx, rx, xs, xr, loc.at[1], me, rep)
    wait_blocks(sy, ry, ys, yr, loc.at[2], me, rep)


def slot_positions(ct):
    me = lax.axis_index("dp")
    table = ct[:, 0, :]
    mine = jnp.where(iota((DP, DP), 1) == me, table, 0).astype(F32)
    counts = jnp.sum(mine, axis=1, keepdims=True)
    source = iota((DP, SLOTS), 0)
    slot_source = iota((DP, SLOTS), 1) // CAP
    start = jnp.sum(jnp.where(source < slot_source, counts, 0.0), axis=0, keepdims=True)
    count = jnp.sum(jnp.where(source == slot_source, counts, 0.0), axis=0, keepdims=True)
    within = lax.rem(iota((1, SLOTS), 1), CAP).astype(F32)
    return jnp.where(within < count, start + within, -1.0)


def compact(pos, rows_ref, out_ref):
    rows = rows_ref[...].reshape(SLOTS, N)
    for chunk in range(2):
        index = (iota((256, SLOTS), 0) + 256 * chunk).astype(F32)
        hot = onehot(index == pos)
        out_ref[256 * chunk : 256 * chunk + 256] = dot(hot, rows).astype(BF16)


def centred(values):
    center = values - jnp.mean(values, axis=-1, keepdims=True)
    spread = jnp.mean(center * center, axis=-1, keepdims=True)
    scale = lax.rsqrt(spread + EPSILON)
    return center * scale, scale


def norm_grad(grad, normed, scale):
    lead = jnp.mean(grad, axis=-1, keepdims=True)
    along = jnp.mean(grad * normed, axis=-1, keepdims=True)
    return scale * (grad - lead - normed * along)


def sigmoid(x):
    return 0.5 * jnp.tanh(0.5 * x) + 0.5


def projection(xh, w, act, slope):
    @pl.loop(0, 8)
    def _(j):
        cols = pl.ds(pl.multiple_of(256 * j, 256), 256)
        pre = dot(xh[...], w[:, cols])
        sig = sigmoid(pre)
        silu = pre * sig
        act[:, cols] = silu.astype(BF16)
        slope[:, cols] = (sig + silu * (1.0 - sig)).astype(BF16)


def allowed_mask(users, mask):
    row = users[...].astype(F32)
    column = column_of(row, N)
    for b in range(4):
        keys = slice(128 * b, 128 * b + 128)
        same = column == row[:, keys]
        causal = iota((N, 128), 1) + 128 * b <= iota((N, 128), 0)
        mask[:, keys] = onehot(same & causal)


def half_lanes(hh):
    return jnp.where(iota((1, 128), 1) // 64 == hh, 1.0, 0.0)


def attention(act, mask, wt, gs, att):
    @pl.loop(0, HEADS // 2)
    def _(p):
        off = pl.multiple_of(128 * p, 128)
        v = act[:, pl.ds(512 + off, 128)]
        q = act[:, pl.ds(1024 + off, 128)]
        k = act[:, pl.ds(1536 + off, 128)]
        for t in range(2):
            rows = slice(256 * t, 256 * t + 256)
            nk = 256 * (t + 1)
            total = None
            for hh in range(2):
                lanes = half_lanes(hh)
                qm = q[rows] * lanes.astype(BF16)
                half = dot_nt(qm, k[:nk]) * 0.0625
                th = jnp.tanh(half)
                silu = half + half * th
                sig = 0.5 + 0.5 * th
                grad = (sig + silu * (1.0 - sig)) * 0.125
                ok = mask[rows, :nk]
                weights = silu.astype(BF16) * ok
                wt[2 * p + hh, rows, :nk] = weights
                gs[2 * p + hh, rows, :nk] = grad.astype(BF16) * ok
                out = dot(weights, v[:nk]) * lanes
                total = out if total is None else total + out
            att[rows, pl.ds(off, 128)] = total


def attention_grad(act, slope, wt, gs, da, dpre):
    @pl.loop(0, HEADS // 2)
    def _(p):
        off = pl.multiple_of(128 * p, 128)
        vcols = pl.ds(512 + off, 128)
        qcols = pl.ds(1024 + off, 128)
        kcols = pl.ds(1536 + off, 128)
        v = act[:, vcols]
        q = act[:, qcols]
        k = act[:, kcols]
        d = da[:, pl.ds(off, 128)]
        qt = jnp.transpose(q)
        dt = jnp.transpose(d)
        dvs, dks = [], []
        dq = [None, None]
        for hh in range(2):
            lanes = half_lanes(hh)
            half = slice(64 * hh, 64 * hh + 64)
            dv, dk = [], []
            for t in range(2):
                rows = slice(256 * t, 256 * t + 256)
                nk = 256 * (t + 1)
                dm = d[rows] * lanes.astype(BF16)
                dw = dot_nt(dm, v[:nk])
                ds = (dw * gs[2 * p + hh, rows, :nk].astype(F32)).astype(BF16)
                part = dot(ds, k[:nk]) * lanes
                dq[t] = part if dq[t] is None else dq[t] + part
                dk.append(dot(qt[half, rows], ds))
                dv.append(dot(dt[half, rows], wt[2 * p + hh, rows, :nk]))
            dks.append(jnp.concatenate([dk[0] + dk[1][:, :256], dk[1][:, 256:]], axis=1))
            dvs.append(jnp.concatenate([dv[0] + dv[1][:, :256], dv[1][:, 256:]], axis=1))
        for t in range(2):
            rows = slice(256 * t, 256 * t + 256)
            dpre[rows, qcols] = dq[t].astype(BF16) * slope[rows, qcols]
        dk = jnp.transpose(jnp.concatenate(dks, axis=0))
        dv = jnp.transpose(jnp.concatenate(dvs, axis=0))
        dpre[:, kcols] = dk.astype(BF16) * slope[:, kcols]
        dpre[:, vcols] = dv.astype(BF16) * slope[:, vcols]


def gate_grad(att, act, slope, dy, wo, da, dpre, gated):
    for t in range(2):
        rows = slice(256 * t, 256 * t + 256)
        normed, scale = centred(att[rows])
        u = act[rows, :N].astype(F32)
        gated[rows] = (normed * u).astype(BF16)
        dg = dot_nt(dy[rows], wo[...]).astype(BF16).astype(F32)
        dpre[rows, :N] = (dg * normed).astype(BF16) * slope[rows, :N]
        da[rows] = norm_grad(dg * u, normed, scale).astype(BF16)


def out_grad(dy, gated, g):
    term = dot(jnp.transpose(dy[...]), gated[...]).astype(BF16)
    term = term.reshape(CHIPS, 2, 16, N)
    for c in range(2):
        for y in range(4):
            g[c, y, :, 64:80, :] = term[:, c, :, 128 * y : 128 * y + 128]


def in_grad(xht, dpre, g):
    @pl.loop(0, 8)
    def _(j):
        cols = pl.ds(pl.multiple_of(256 * j, 256), 256)
        term = dot(xht[...], dpre[:, cols]).astype(BF16)
        for half in range(2):
            for c in range(2):
                for y in range(4):
                    first = 256 * c + 64 * y
                    g[c, y, 2 * j + half, 0:64, :] = term[
                        first : first + 64, 128 * half : 128 * half + 128
                    ]


def row_grad(x, dy, dpre, w, dx):
    for t in range(2):
        rows = slice(256 * t, 256 * t + 256)
        dxh = dot_nt(dpre[rows], w[...]).astype(BF16).astype(F32)
        normed, scale = centred(x[rows].astype(F32))
        dx[rows] = (norm_grad(dxh, normed, scale) + dy[rows].astype(F32)).astype(BF16)


def spread(pos, dx, out):
    column = column_of(pos, SLOTS)
    for chunk in range(4):
        part = column[256 * chunk : 256 * chunk + 256]
        hot = jnp.concatenate(
            [onehot((iota((256, 128), 1) + 128 * b).astype(F32) == part) for b in range(4)],
            axis=1,
        )
        out[8 * chunk : 8 * chunk + 8] = dot(hot, dx[...]).astype(BF16).reshape(8, CAP, N)


def layer_kernel(
    rx, ry, ct, users, w, wo, dxp, g, x, dy, xh, xht, act, slope, mask, wt, gs, att, da, dpre, gated, dx
):
    pos = slot_positions(ct)
    compact(pos, rx, x)
    xh[...] = centred(x[...].astype(F32))[0].astype(BF16)
    xht[...] = jnp.transpose(xh[...])
    projection(xh, w, act, slope)
    allowed_mask(users, mask)
    attention(act, mask, wt, gs, att)
    compact(pos, ry, dy)
    gate_grad(att, act, slope, dy, wo, da, dpre, gated)
    out_grad(dy, gated, g)
    attention_grad(act, slope, wt, gs, da, dpre)
    in_grad(xht, dpre, g)
    row_grad(x, dy, dpre, w, dx)
    spread(pos, dx, dxp)


LAYER_SCRATCH = [
    pltpu.VMEM((N, N), BF16),
    pltpu.VMEM((N, N), BF16),
    pltpu.VMEM((N, N), BF16),
    pltpu.VMEM((N, N), BF16),
    pltpu.VMEM((N, 4 * N), BF16),
    pltpu.VMEM((N, 4 * N), BF16),
    pltpu.VMEM((N, N), BF16),
    pltpu.VMEM((HEADS, N, N), BF16),
    pltpu.VMEM((HEADS, N, N), BF16),
    pltpu.VMEM((N, N), F32),
    pltpu.VMEM((N, N), BF16),
    pltpu.VMEM((N, 4 * N), BF16),
    pltpu.VMEM((N, N), BF16),
    pltpu.VMEM((N, N), BF16),
]


def collect_kernel(
    dxp, g, place, ge, gw, gout,
    ret, r1, s1, r2, s2, r3, s3, r4, hot,
    bs, br, s1s, s1r, s2s, s2r, s3s, s3r, s4s, s4r, loc,
):
    me, rep = position()
    core = lax.rem(me, 2)
    chip = me // 2
    partner = chip * 2 + (1 - core)
    barrier = pltpu.get_barrier_semaphore()
    group_signal(barrier, me, rep)
    for i in range(1, REP):
        for c in range(2):
            pl.semaphore_signal(
                barrier, 1, device_id=(chip * 2 + c, lax.rem(rep + i, REP)), device_id_type=MESH
            )
    column = column_of(place[...].astype(F32), N)
    for b in range(8):
        hot[:, 128 * b : 128 * b + 128] = onehot(
            (iota((N, 128), 1) + 128 * b).astype(F32) == column
        )
    pl.semaphore_wait(barrier, DP - 1 + 2 * (REP - 1))

    def first(i):
        y = lax.rem(rep + i, REP)
        return y, remote(g.at[1 - core, y], r1.at[y], s1s.at[i], s1r.at[i], partner, rep)

    for i in (2, 1, 3, 0):
        first(i)[1].start()
    send_blocks(dxp, ret, bs, br, loc, me, rep)

    def second(i):
        y = lax.rem(rep + i, REP)
        return remote(s1.at[y], r2.at[i], s2s.at[i], s2r.at[i], me, y)

    for i in (2, 1, 3, 0):
        y, copy = first(i)
        copy.wait()
        s1[y] = (g[core, y].astype(F32) + r1[y].astype(F32)).astype(BF16)
        if i:
            second(i).start()
    for i in (2, 1, 3):
        second(i).wait()
    s2[...] = (
        s1[rep].astype(F32) + r2[1].astype(F32) + r2[2].astype(F32) + r2[3].astype(F32)
    ).astype(BF16)

    def third(i, mine):
        other = lax.rem(chip + i, CHIPS)
        place_in = chip if mine else other
        return remote(
            s2.at[other], r3.at[place_in], s3s.at[other], s3r.at[place_in], other * 2 + core, rep
        )

    @pl.loop(1, CHIPS)
    def _(i):
        third(i, True).start()

    @pl.loop(1, CHIPS)
    def _(i):
        third(i, False).wait()

    r3[chip] = s2[chip]
    total = r3[0].astype(F32)
    for i in range(1, CHIPS):
        total = total + r3[i].astype(F32)
    s3[...] = total.astype(BF16)

    def fourth(i, c, mine):
        y = lax.rem(rep + i, REP)
        other = c if c is not None else core
        to = chip * 2 + (1 - core if c else core)
        from_y, from_c = (rep, core) if mine else (y, 1 - core if c else core)
        slot = from_y * 2 + from_c
        to_slot = y * 2 + (1 - core if c else core)
        del other
        return remote(s3, r4.at[slot], s4s.at[to_slot], s4r.at[slot], to, y)

    for i in range(REP):
        for c in (0, 1):
            if i or c:
                fourth(i, c, True).start()
    r4[rep * 2 + core] = s3[...]
    for i in range(REP):
        for c in (0, 1):
            if i or c:
                fourth(i, c, False).wait()
    for y in range(4):
        for c in range(2):
            block = r4[y * 2 + c, 0:64, :].astype(F32)
            block = jnp.where(core == 1, pltpu.roll(block, 64, 1), block)
            gw[256 * c + 64 * y : 256 * c + 64 * y + 64, :] = block[:, :64]
        tail = r4[y * 2 + core, 64:80, :].astype(F32)
        tail = jnp.concatenate([tail, jnp.zeros((112, 128), F32)], axis=0)
        gout[128 * y : 128 * y + 128, :] = jnp.transpose(tail)[:, :16]
    wait_blocks(dxp, ret, bs, br, loc, me, rep)
    rows = ret[...].reshape(SLOTS, N)
    ge[...] = dot(hot[...], rows).astype(BF16)


DMA = pltpu.SemaphoreType.DMA
COLLECT_SCRATCH = [
    pltpu.VMEM((DP, CAP, N), BF16),
    pltpu.VMEM((4, CHIPS, 80, 128), BF16),
    pltpu.VMEM((4, CHIPS, 80, 128), BF16),
    pltpu.VMEM((4, CHIPS, 80, 128), BF16),
    pltpu.VMEM((CHIPS, 80, 128), BF16),
    pltpu.VMEM((CHIPS, 80, 128), BF16),
    pltpu.VMEM((80, 128), BF16),
    pltpu.VMEM((8, 80, 128), BF16),
    pltpu.VMEM((N, SLOTS), BF16),
    DMA((DP,)), DMA((DP,)), DMA((4,)), DMA((4,)), DMA((4,)), DMA((4,)),
    DMA((CHIPS,)), DMA((CHIPS,)), DMA((8,)), DMA((8,)), DMA,
]

BUFFER = jax.ShapeDtypeStruct((DP, CAP, N), BF16)
VM = pl.BlockSpec(memory_space=pltpu.VMEM)


def on_device(events, grad_out, w_uvqk, w_out, send_place, send_counts, user_ids):
    rx, ry, ct = pl.pallas_call(
        dispatch_kernel,
        name="dispatch",
        out_shape=(BUFFER, BUFFER, jax.ShapeDtypeStruct((DP, 1, DP), I32)),
        in_specs=[VM] * 4,
        out_specs=(VM,) * 3,
        scratch_shapes=[
            pltpu.VMEM((DP, CAP, N), BF16), pltpu.VMEM((DP, CAP, N), BF16),
            DMA((DP,)), DMA((DP,)), DMA((DP,)), DMA((DP,)), DMA((DP,)), DMA((DP,)), DMA((3,)),
        ],
        compiler_params=pltpu.CompilerParams(
            collective_id=0, has_side_effects=True, vmem_limit_bytes=VMEM_LIMIT
        ),
    )(events, grad_out, send_place, send_counts)
    dxp, g = pl.pallas_call(
        layer_kernel,
        name="layer",
        out_shape=(BUFFER, jax.ShapeDtypeStruct((2, 4, CHIPS, 80, 128), BF16)),
        in_specs=[VM] * 6,
        out_specs=(VM,) * 2,
        scratch_shapes=LAYER_SCRATCH,
        compiler_params=pltpu.CompilerParams(vmem_limit_bytes=VMEM_LIMIT),
    )(rx, ry, ct, user_ids, w_uvqk, w_out)
    ge, gw, gout = pl.pallas_call(
        collect_kernel,
        name="collect",
        out_shape=(
            jax.ShapeDtypeStruct((N, N), BF16),
            jax.ShapeDtypeStruct((N, 64), F32),
            jax.ShapeDtypeStruct((N, 16), F32),
        ),
        in_specs=[VM] * 3,
        out_specs=(VM,) * 3,
        scratch_shapes=COLLECT_SCRATCH,
        compiler_params=pltpu.CompilerParams(
            collective_id=1, has_side_effects=True, vmem_limit_bytes=VMEM_LIMIT
        ),
    )(dxp, g, send_place)
    return ge, gw, gout


def solution(mesh):
    rows = P(("dp", "rep"), None)
    return jax.shard_map(
        on_device,
        mesh=mesh,
        in_specs=(rows, rows, P(), P(), rows, rows, rows),
        out_specs=(rows, P(None, "dp"), P(None, "dp")),
        check_vma=False,
    )
```

time: 395 us -> 111 us (0.28)
  the two profiles are of different devices: /device:TPU:0 before, /device:TPU:1 now
where the time goes in v1:
time: 111 us; the launch traced here: 110 us
  Pallas kernels  105 us (95%)
  local copies, waits for them, and re-layouts  5.26 us (5%)
    pallas_call x1, Pallas kernels, on_device(): pl.pallas_call(collect_kernel, name='collect', out_shape=(jax.ShapeDtypeS...  41.2 us
    pallas_call x1, Pallas kernels, on_device(): pl.pallas_call(dispatch_kernel, name='dispatch', out_shape=(BUFFER, BUFFE...  39.3 us
    pallas_call x1, Pallas kernels, on_device(): pl.pallas_call(layer_kernel, name='layer', out_shape=(BUFFER, jax.ShapeDt...  23.9 us
    pallas_call x2, local copies, waits for them, and re-layouts, on_device(): pl.pallas_call(collect_kernel, name='collect', out_shape=(jax.ShapeDtypeS...  3.39 us

profile of v1, /device:TPU:1, one launch (start us, length us, event | category | flops | bytes accessed | tf_op | source)
XLA Modules:
  0.0 110.4 jit_solution(5555276119205231791)
XLA Ops:
  0.6 39.3 %dispatch.1 = (bf16[32,32,512]{2,1,0:T(8,128)(2,1)}, bf16[32,32,512]{2,1,0:T(8,128)(2,1)}, s32[32,1,32]{2,1,0:T(1,128)}) custom-call(bf16[512,512]{1,0:T(8,128)(2,1)} %ev.1, bf16[512,512]{1,0:T(8,128)(2,1)} %go.1, s32[1,512]{1,0:T(1,128)} %place.3, s32[1,32]{1,0:T(1,128)} %cnt.1), custom_call_target="tpu_custom_call" | custom-call | tf_op jit(solution)/shard_map/dispatch/pallas_call | solution.py:468
  40.0 23.9 %layer.1 = (bf16[32,32,512]{2,1,0:T(8,128)(2,1)}, bf16[2,4,16,80,128]{4,3,2,1,0:T(8,128)(2,1)}) custom-call(bf16[32,32,512]{2,1,0:T(8,128)(2,1)} %get-tuple-element.8.rx, bf16[32,32,512]{2,1,0:T(8,128)(2,1)} %get-tuple-element.9.ry, s32[32,1,32]{2,1,0:T(1,128)} %get-tuple-element.10.ct, s32[1,512]{1,0:T(1,128)} %users.1, bf16[512,2048]{1,0:T(8,128)(2,1)} %w.1, ...), custom_call_target="tpu_custom_call" | custom-call | tf_op jit(solution)/shard_map/layer/pallas_call | solution.py:482
  63.9 41.2 %collect.1 = (bf16[512,512]{1,0:T(8,128)(2,1)}, f32[512,64]{1,0:T(8,128)}, f32[512,16]{1,0:T(8,128)}) custom-call(bf16[32,32,512]{2,1,0:T(8,128)(2,1)} %get-tuple-element.11.dxp, bf16[2,4,16,80,128]{4,3,2,1,0:T(8,128)(2,1)} %get-tuple-element.12.g, s32[1,512]{1,0:T(1,128)} %place.3), custom_call_target="tpu_custom_call" | custom-call | tf_op jit(solution)/shard_map/collect/pallas_call | solution.py:491
  105.2 1.7 %copy.11 = f32[512,16]{0,1:T(8,128)} copy(f32[512,16]{1,0:T(8,128)} %get-tuple-element.15) | data formatting | bytes 65536 | tf_op jit(solution)/shard_map/collect/pallas_call | solution.py:491
  106.8 1.7 %copy.10 = f32[512,64]{0,1:T(8,128)} copy(f32[512,64]{1,0:T(8,128)} %get-tuple-element.14) | data formatting | bytes 262144 | tf_op jit(solution)/shard_map/collect/pallas_call | solution.py:491
  108.6 1.9 %copy.13 = bf16[512,512]{1,0:T(8,128)(2,1)} copy(bf16[512,512]{1,0:T(8,128)(2,1)} %get-tuple-element.19) | data formatting | bytes 1048576

commit v2 on v0

v2 whole, which is shorter than its diff:
```python
import jax
import jax.numpy as jnp
from jax import lax
from jax.experimental import pallas as pl
from jax.experimental.pallas import tpu as pltpu
from jax.sharding import PartitionSpec as P

HEADS = 8
EPSILON = 1e-05
F32 = jnp.float32
BF16 = jnp.bfloat16
I32 = jnp.int32
MESH = pl.DeviceIdType.MESH
N = 512
DP = 32
REP = 4
CAP = 32
SLOTS = 1024
CHIPS = 16
VMEM_LIMIT = 62 * 1024 * 1024


def dot(a, b):
    return jnp.dot(a, b, preferred_element_type=F32)


def dot_nt(a, b):
    return lax.dot_general(a, b, (((1,), (1,)), ((), ())), preferred_element_type=F32)


def iota(shape, dim):
    return lax.broadcasted_iota(I32, shape, dim)


def onehot(mask):
    return jnp.where(mask, 1.0, 0.0).astype(BF16)


def column_of(row, width):
    return jnp.transpose(jnp.broadcast_to(row, (128, width)))


def remote(src, dst, send, recv, dp, rep):
    return pltpu.make_async_remote_copy(
        src_ref=src,
        dst_ref=dst,
        send_sem=send,
        recv_sem=recv,
        device_id=(dp, rep),
        device_id_type=MESH,
    )


def signal(barrier, dp, rep):
    pl.semaphore_signal(barrier, 1, device_id=(dp, rep), device_id_type=MESH)


class Place:
    def __init__(self):
        self.me = lax.axis_index("dp")
        self.rep = lax.axis_index("rep")
        self.core = lax.rem(self.me, 2)
        self.chip = self.me // 2
        self.x = self.me // 8
        self.z = lax.rem(self.chip, 4)
        self.partner = self.chip * 2 + (1 - self.core)


def pack(place, rows, out):
    for chunk in range(4):
        hot = onehot(iota((256, N), 0) + 256 * chunk == place)
        out[8 * chunk : 8 * chunk + 8] = dot(hot, rows).astype(BF16).reshape(8, CAP, N)


def each_peer(at, dx, body):
    column = lax.rem(at.x + dx, 4) * 8
    inner = lax.rem(at.me, 8)

    @pl.loop(0 if dx else 1, 8)
    def _(j):
        body(column + lax.rem(inner + j, 8))


class Exchange:
    def __init__(self, at, src, dst, send, recv, local, whole=False):
        self.at, self.src, self.dst = at, src, dst
        self.sems, self.local, self.whole = (send, recv), local, whole

    def block(self, peer):
        return self.src if self.whole else self.src.at[peer]

    def own(self):
        me = self.at.me
        return pltpu.make_async_copy(self.block(me), self.dst.at[me], self.local)

    def start(self, dx):
        at, (send, recv) = self.at, self.sems

        def body(peer):
            remote(
                self.block(peer), self.dst.at[at.me], send.at[peer], recv.at[at.me], peer, at.rep
            ).start()

        each_peer(at, dx, body)
        if dx == 0:
            self.own().start()

    def start_all(self):
        for dx in (2, 1, 3, 0):
            self.start(dx)

    def wait(self):
        at, (send, recv) = self.at, self.sems

        def body(peer):
            remote(
                self.block(peer), self.dst.at[peer], send.at[peer], recv.at[peer], peer, at.rep
            ).wait()

        for dx in (0, 1, 3, 2):
            each_peer(at, dx, body)
        self.own().wait()


class Reduce:
    def __init__(self, at, g, r1, s1, r2, s2, r3, r3w, s3, r4, sems):
        self.at = at
        self.g, self.r1, self.s1, self.r2, self.s2 = g, r1, s1, r2, s2
        self.r3, self.r3w, self.s3, self.r4 = r3, r3w, s3, r4
        (self.a_s, self.a_r, self.b_s, self.b_r, self.c_s, self.c_r,
         self.w_s, self.w_r, self.d_s, self.d_r) = sems

    def pair(self, s):
        at = self.at
        return remote(
            self.g.at[1 - at.core, s], self.r1.at[s], self.a_s.at[s], self.a_r.at[s], at.partner, at.rep
        )

    def over_y(self, s, i):
        at = self.at
        y = lax.rem(at.rep + i, REP)
        return remote(
            self.s1.at[s, y], self.r2.at[s, i], self.b_s.at[s, i], self.b_r.at[s, i], at.me, y
        )

    def pair_done(self, s):
        at = self.at
        self.pair(s).wait()
        self.s1[s] = (self.g[at.core, s].astype(F32) + self.r1[s].astype(F32)).astype(BF16)
        for i in (2, 1, 3):
            self.over_y(s, i).start()

    def y_done(self, s):
        for i in (2, 1, 3):
            self.over_y(s, i).wait()
        total = self.s1[s, self.at.rep].astype(F32)
        for i in (1, 2, 3):
            total = total + self.r2[s, i].astype(F32)
        self.s2[s] = total.astype(BF16)

    def column(self, p, x, slot):
        at = self.at
        to = x * 4 + p
        return remote(
            self.s2.at[1 + p, pl.ds(64 * x, 64)], self.r3.at[slot],
            self.c_s.at[p, x], self.c_r.at[slot], to * 2 + at.core, at.rep,
        )

    def columns_start(self, p):
        at = self.at
        for x in range(4):

            @pl.when(x * 4 + p != at.chip)
            def _():
                self.column(p, x, at.chip).start()

    def out_rows(self, other, slot):
        at = self.at
        return remote(
            self.s2.at[0, pl.ds(pl.multiple_of(16 * other, 16), 16)], self.r3w.at[slot],
            self.w_s.at[other], self.w_r.at[slot], other * 2 + at.core, at.rep,
        )

    def out_start(self):
        @pl.loop(1, CHIPS)
        def _(i):
            self.out_rows(lax.rem(self.at.chip + i, CHIPS), self.at.chip).start()

    def gather(self, i, other_core, mine):
        at = self.at
        y = lax.rem(at.rep + i, REP)
        core = 1 - at.core if other_core else at.core
        slot = at.rep * 2 + at.core if mine else y * 2 + core
        return remote(
            self.s3, self.r4.at[slot], self.d_s.at[y * 2 + core], self.d_r.at[slot], at.chip * 2 + core, y
        )

    def finish(self):
        at = self.at

        @pl.loop(1, CHIPS)
        def _(i):
            other = lax.rem(at.chip + i, CHIPS)
            self.out_rows(other, other).wait()
            remote(
                self.r3.at[other], self.r3.at[other], self.d_s.at[0], self.c_r.at[other], other * 2 + at.core, at.rep
            ).wait_recv()

        for p in range(4):
            for x in range(4):

                @pl.when(x * 4 + p != at.chip)
                def _(p=p, x=x):
                    self.column(p, x, at.chip).wait_send()

        self.r3[at.chip] = self.s2[1 + at.z, pl.ds(pl.multiple_of(64 * at.x, 64), 64)]
        self.r3w[at.chip] = self.s2[0, pl.ds(pl.multiple_of(16 * at.chip, 16), 16)]
        for ref, rows in ((self.r3, slice(0, 64)), (self.r3w, slice(64, 80))):
            total = ref[0].astype(F32)
            for i in range(1, CHIPS):
                total = total + ref[i].astype(F32)
            self.s3[rows] = total.astype(BF16)
        order = [(i, other) for i in (2, 1, 3, 0) for other in (True, False) if i or other]
        for i, other in order:
            self.gather(i, other, True).start()
        self.r4[at.rep * 2 + at.core] = self.s3[...]
        for i, other in order:
            self.gather(i, other, False).wait()


def slot_positions(ct):
    me = lax.axis_index("dp")
    table = ct[:, 0, :]
    mine = jnp.where(iota((DP, DP), 1) == me, table, 0).astype(F32)
    counts = jnp.sum(mine, axis=1, keepdims=True)
    source = iota((DP, SLOTS), 0)
    slot_source = iota((DP, SLOTS), 1) // CAP
    start = jnp.sum(jnp.where(source < slot_source, counts, 0.0), axis=0, keepdims=True)
    count = jnp.sum(jnp.where(source == slot_source, counts, 0.0), axis=0, keepdims=True)
    within = lax.rem(iota((1, SLOTS), 1), CAP).astype(F32)
    return jnp.where(within < count, start + within, -1.0)


def compact(pos, rows_ref, out_ref):
    rows = rows_ref[...].reshape(SLOTS, N)
    for chunk in range(2):
        index = (iota((256, SLOTS), 0) + 256 * chunk).astype(F32)
        hot = onehot(index == pos)
        out_ref[256 * chunk : 256 * chunk + 256] = dot(hot, rows).astype(BF16)


def centred(values):
    center = values - jnp.mean(values, axis=-1, keepdims=True)
    spread = jnp.mean(center * center, axis=-1, keepdims=True)
    scale = lax.rsqrt(spread + EPSILON)
    return center * scale, scale


def norm_grad(grad, normed, scale):
    lead = jnp.mean(grad, axis=-1, keepdims=True)
    along = jnp.mean(grad * normed, axis=-1, keepdims=True)
    return scale * (grad - lead - normed * along)


def sigmoid(x):
    return 0.5 * jnp.tanh(0.5 * x) + 0.5


def allowed_mask(users, mask):
    row = users[...].astype(F32)
    column = column_of(row, N)
    for b in range(4):
        keys = slice(128 * b, 128 * b + 128)
        same = column == row[:, keys]
        causal = iota((N, 128), 1) + 128 * b <= iota((N, 128), 0)
        mask[:, keys] = onehot(same & causal)


def half_lanes(hh):
    return jnp.where(iota((1, 128), 1) // 64 == hh, 1.0, 0.0)


U, V, Q, K = (slice(128 * i, 128 * i + 128) for i in range(4))


def pair_forward(p, xh, wp, mask, act, slope, wt, gs, att):
    for half in range(2):
        cols = slice(256 * half, 256 * half + 256)
        pre = dot(xh[...], wp[p, :, cols])
        sig = sigmoid(pre)
        silu = pre * sig
        act[p, :, cols] = silu.astype(BF16)
        slope[p, :, cols] = (sig + silu * (1.0 - sig)).astype(BF16)
    v, q, k = act[p, :, V], act[p, :, Q], act[p, :, K]
    for t in range(2):
        rows = slice(256 * t, 256 * t + 256)
        nk = 256 * (t + 1)
        total = None
        for hh in range(2):
            lanes = half_lanes(hh)
            qm = q[rows] * lanes.astype(BF16)
            half = dot_nt(qm, k[:nk]) * 0.0625
            th = jnp.tanh(half)
            silu = half + half * th
            sig = 0.5 + 0.5 * th
            grad = (sig + silu * (1.0 - sig)) * 0.125
            ok = mask[rows, :nk]
            weights = silu.astype(BF16) * ok
            wt[2 * p + hh, rows, :nk] = weights
            gs[2 * p + hh, rows, :nk] = grad.astype(BF16) * ok
            out = dot(weights, v[:nk]) * lanes
            total = out if total is None else total + out
        att[rows, pl.ds(pl.multiple_of(128 * p, 128), 128)] = total


def pair_backward(p, act, slope, wt, gs, da, dpre):
    v, q, k = act[p, :, V], act[p, :, Q], act[p, :, K]
    d = da[:, pl.ds(pl.multiple_of(128 * p, 128), 128)]
    qt = jnp.transpose(q)
    dt = jnp.transpose(d)
    dvs, dks = [], []
    dq = [None, None]
    for hh in range(2):
        lanes = half_lanes(hh)
        half = slice(64 * hh, 64 * hh + 64)
        dv, dk = [], []
        for t in range(2):
            rows = slice(256 * t, 256 * t + 256)
            nk = 256 * (t + 1)
            dm = d[rows] * lanes.astype(BF16)
            dw = dot_nt(dm, v[:nk])
            ds = (dw * gs[2 * p + hh, rows, :nk].astype(F32)).astype(BF16)
            part = dot(ds, k[:nk]) * lanes
            dq[t] = part if dq[t] is None else dq[t] + part
            dk.append(dot(qt[half, rows], ds))
            dv.append(dot(dt[half, rows], wt[2 * p + hh, rows, :nk]))
        dks.append(jnp.concatenate([dk[0] + dk[1][:, :256], dk[1][:, 256:]], axis=1))
        dvs.append(jnp.concatenate([dv[0] + dv[1][:, :256], dv[1][:, 256:]], axis=1))
    for t in range(2):
        rows = slice(256 * t, 256 * t + 256)
        dpre[p, rows, Q] = dq[t].astype(BF16) * slope[p, rows, Q]
    dk = jnp.transpose(jnp.concatenate(dks, axis=0))
    dv = jnp.transpose(jnp.concatenate(dvs, axis=0))
    dpre[p, :, K] = dk.astype(BF16) * slope[p, :, K]
    dpre[p, :, V] = dv.astype(BF16) * slope[p, :, V]


def gate_grad(att, act, slope, dy, wo, da, dpre, gated):
    for t in range(2):
        rows = slice(256 * t, 256 * t + 256)
        normed, scale = centred(att[rows])
        u = jnp.concatenate([act[p, rows, U] for p in range(4)], axis=1).astype(F32)
        gated[rows] = (normed * u).astype(BF16)
        dg = dot_nt(dy[rows], wo[...]).astype(BF16).astype(F32)
        du = (dg * normed).astype(BF16)
        for p in range(4):
            dpre[p, rows, U] = du[:, 128 * p : 128 * p + 128] * slope[p, rows, U]
        da[rows] = norm_grad(dg * u, normed, scale).astype(BF16)


def out_grad(dy, gated, g):
    term = dot(jnp.transpose(dy[...]), gated[...]).astype(BF16)
    term = term.reshape(CHIPS, 2, 16, N)
    for c in range(2):
        for y in range(4):
            g[c, 0, y] = term[:, c, :, 128 * y : 128 * y + 128].reshape(256, 128)


def pair_in_grad(p, xht, dpre, g):
    for half in range(2):
        term = dot(xht[...], dpre[p, :, 256 * half : 256 * half + 256]).astype(BF16)
        for x in range(2):
            for c in range(2):
                for y in range(4):
                    first = 256 * c + 64 * y
                    row = 64 * (2 * half + x)
                    g[c, 1 + p, y, row : row + 64, :] = term[
                        first : first + 64, 128 * x : 128 * x + 128
                    ]


def row_grad(x, dy, dpre, wp, dx):
    for t in range(2):
        rows = slice(256 * t, 256 * t + 256)
        dxh = dot_nt(dpre[0, rows], wp[0])
        for p in range(1, 4):
            dxh = dxh + dot_nt(dpre[p, rows], wp[p])
        dxh = dxh.astype(BF16).astype(F32)
        normed, scale = centred(x[rows].astype(F32))
        dx[rows] = (norm_grad(dxh, normed, scale) + dy[rows].astype(F32)).astype(BF16)


def spread(chunk, column, dx, out):
    part = column[pl.ds(pl.multiple_of(256 * chunk, 256), 256)]
    hot = jnp.concatenate(
        [onehot((iota((256, 128), 1) + 128 * b).astype(F32) == part) for b in range(4)], axis=1
    )
    out[pl.ds(8 * chunk, 8)] = dot(hot, dx[...]).astype(BF16).reshape(8, CAP, N)


def layer_kernel(
    ev_any, go_any, w_any, wo_any, place, cnt, users,
    ret, r4,
    ev, go, wp, wo, sx, sy, rx, ry, ct, dxp,
    x, dy, xh, xht, act, slope, mask, wt, gs, att, da, dpre, gated, dx, column,
    g, r1, s1, r2, s2, r3, r3w, s3,
    xs, xr, ys, yr, cs, cr, bs, br, loc, load,
    a_s, a_r, b_s, b_r, c_s, c_r, w_s, w_r, d_s, d_r,
):
    at = Place()
    barrier = pltpu.get_barrier_semaphore()
    for dxo in range(4):
        each_peer(at, dxo, lambda peer: signal(barrier, peer, at.rep))
    for i in range(1, REP):
        for c in range(2):
            signal(barrier, at.chip * 2 + c, lax.rem(at.rep + i, REP))
    loads = [pltpu.make_async_copy(ev_any, ev, load.at[0]), pltpu.make_async_copy(go_any, go, load.at[1])]
    for p in range(4):
        for i in range(4):
            loads.append(
                pltpu.make_async_copy(
                    w_any.at[:, pl.ds(512 * i + 128 * p, 128)],
                    wp.at[p, :, pl.ds(128 * i, 128)],
                    load.at[2 + 4 * p + i],
                )
            )
    loads.append(pltpu.make_async_copy(wo_any, wo, load.at[18]))
    for copy in loads:
        copy.start()
    loads[0].wait()
    pack(place[...], ev[...], sx)
    to_x = Exchange(at, sx, rx, xs, xr, loc.at[0])
    to_y = Exchange(at, sy, ry, ys, yr, loc.at[1])
    counts = Exchange(at, cnt, ct, cs, cr, loc.at[2], whole=True)
    back = Exchange(at, dxp, ret, bs, br, loc.at[3])
    reduce = Reduce(
        at, g, r1, s1, r2, s2, r3, r3w, s3, r4,
        (a_s, a_r, b_s, b_r, c_s, c_r, w_s, w_r, d_s, d_r),
    )
    pl.semaphore_wait(barrier, DP - 1 + 2 * (REP - 1))
    counts.start_all()
    to_x.start_all()
    loads[1].wait()
    pack(place[...], go[...], sy)
    to_y.start_all()
    allowed_mask(users, mask)
    counts.wait()
    pos = slot_positions(ct)
    column[...] = column_of(pos, SLOTS)
    for copy in loads[2:]:
        copy.wait()
    to_x.wait()
    compact(pos, rx, x)
    xh[...] = centred(x[...].astype(F32))[0].astype(BF16)
    xht[...] = jnp.transpose(xh[...])

    @pl.loop(0, 4)
    def _(p):
        pair_forward(p, xh, wp, mask, act, slope, wt, gs, att)

    to_y.wait()
    compact(pos, ry, dy)
    gate_grad(att, act, slope, dy, wo, da, dpre, gated)
    out_grad(dy, gated, g)
    reduce.pair(0).start()

    @pl.loop(0, 4)
    def _(p):
        pair_backward(p, act, slope, wt, gs, da, dpre)
        pair_in_grad(p, xht, dpre, g)
        reduce.pair(1 + p).start()
        reduce.pair_done(p)

        @pl.when(p >= 1)
        def _():
            reduce.y_done(p - 1)

    reduce.out_start()
    for p in range(2):
        reduce.columns_start(p)
    row_grad(x, dy, dpre, wp, dx)
    reduce.pair_done(4)
    reduce.y_done(3)
    reduce.columns_start(2)
    for dxo in (2, 1, 3):
        spread(lax.rem(at.x + dxo, 4), column, dx, dxp)
        back.start(dxo)
    spread(at.x, column, dx, dxp)
    reduce.y_done(4)
    reduce.columns_start(3)
    back.start(0)
    reduce.finish()
    back.wait()


def finish_kernel(ret, r4, place, ge, gw, gout):
    core = lax.rem(lax.axis_index("dp"), 2)
    column = column_of(place[...].astype(F32), N)
    hot = jnp.concatenate(
        [onehot((iota((N, 128), 1) + 128 * b).astype(F32) == column) for b in range(8)], axis=1
    )
    ge[...] = dot(hot, ret[...].reshape(SLOTS, N)).astype(BF16)
    for c in range(2):
        for half in range(2):
            block = jnp.concatenate([r4[4 * half + c, :64], r4[4 * half + 2 + c, :64]], axis=0)
            block = jnp.transpose(block.astype(F32))
            first = 256 * c + 128 * half
            gw[:, first : first + 128] = jnp.where(core == 1, block[64:], block[:64])
    for y in range(4):
        gout[:, 128 * y : 128 * y + 128] = r4[2 * y + core, 64:80].astype(F32)


DMA = pltpu.SemaphoreType.DMA
BLOCKS = pltpu.VMEM((DP, CAP, N), BF16)
SQUARE = pltpu.VMEM((N, N), BF16)
PAIRS = pltpu.VMEM((4, N, N), BF16)
TERMS = pltpu.VMEM((5, 4, 256, 128), BF16)
SCRATCH = [
    SQUARE, SQUARE, PAIRS, SQUARE,
    BLOCKS, BLOCKS, BLOCKS, BLOCKS, pltpu.VMEM((DP, 1, DP), I32), BLOCKS,
    SQUARE, SQUARE, SQUARE, SQUARE, PAIRS, PAIRS, SQUARE,
    pltpu.VMEM((HEADS, N, N), BF16), pltpu.VMEM((HEADS, N, N), BF16),
    pltpu.VMEM((N, N), F32), SQUARE, PAIRS, SQUARE, SQUARE,
    pltpu.VMEM((SLOTS, 128), F32),
    pltpu.VMEM((2, 5, 4, 256, 128), BF16), TERMS, TERMS, TERMS,
    pltpu.VMEM((5, 256, 128), BF16),
    pltpu.VMEM((CHIPS, 64, 128), BF16), pltpu.VMEM((CHIPS, 16, 128), BF16),
    pltpu.VMEM((80, 128), BF16),
    DMA((DP,)), DMA((DP,)), DMA((DP,)), DMA((DP,)), DMA((DP,)), DMA((DP,)), DMA((DP,)), DMA((DP,)),
    DMA((4,)), DMA((19,)),
    DMA((5,)), DMA((5,)), DMA((5, 4)), DMA((5, 4)), DMA((4, 4)), DMA((CHIPS,)),
    DMA((CHIPS,)), DMA((CHIPS,)), DMA((8,)), DMA((8,)),
]
VM = pl.BlockSpec(memory_space=pltpu.VMEM)
ANY = pl.BlockSpec(memory_space=pl.ANY)


def on_device(events, grad_out, w_uvqk, w_out, send_place, send_counts, user_ids):
    ret, r4 = pl.pallas_call(
        layer_kernel,
        name="layer",
        out_shape=(
            jax.ShapeDtypeStruct((DP, CAP, N), BF16),
            jax.ShapeDtypeStruct((8, 80, 128), BF16),
        ),
        in_specs=[ANY] * 4 + [VM] * 3,
        out_specs=(VM,) * 2,
        scratch_shapes=SCRATCH,
        compiler_params=pltpu.CompilerParams(
            collective_id=0, has_side_effects=True, vmem_limit_bytes=VMEM_LIMIT
        ),
    )(events, grad_out, w_uvqk, w_out, send_place, send_counts, user_ids)
    ge, gw, gout = pl.pallas_call(
        finish_kernel,
        name="finish",
        out_shape=(
            jax.ShapeDtypeStruct((N, N), BF16),
            jax.ShapeDtypeStruct((64, N), F32),
            jax.ShapeDtypeStruct((16, N), F32),
        ),
        in_specs=[VM] * 3,
        out_specs=(VM,) * 3,
        compiler_params=pltpu.CompilerParams(vmem_limit_bytes=32 * 1024 * 1024),
    )(ret, r4, send_place)
    return ge, gw.T, gout.T


def solution(mesh):
    rows = P(("dp", "rep"), None)
    return jax.shard_map(
        on_device,
        mesh=mesh,
        in_specs=(rows, rows, P(), P(), rows, rows, rows),
        out_specs=(rows, P(None, "dp"), P(None, "dp")),
        check_vma=False,
    )
```

time: 395 us -> 84 us (0.21)
  the two profiles are of different devices: /device:TPU:0 before, /device:TPU:96 now
where the time goes in v2:
time: 84 us; the launch traced here: 83.8 us
  Pallas kernels  81 us (96%)
  local copies, waits for them, and re-layouts  2.14 us (3%)
    pallas_call x1, Pallas kernels, on_device(): pl.pallas_call(layer_kernel, name='layer', out_shape=(jax.ShapeDtypeStruc...  79.5 us
    unnamed x6, local copies, waits for them, and re-layouts  2.14 us

profile of v2, /device:TPU:96, one launch (start us, length us, event | category | flops | bytes accessed | tf_op | source)
XLA Modules:
  0.0 83.8 jit_solution(1730061040586293672)
XLA Ops:
  0.6 0.0 copy-start.2
  0.6 79.5 %layer.1 = (bf16[32,32,512]{2,1,0:T(8,128)(2,1)}, bf16[8,80,128]{2,1,0:T(8,128)(2,1)}) custom-call(bf16[512,512]{1,0:T(8,128)(2,1)} %ev_any.1, bf16[512,512]{1,0:T(8,128)(2,1)} %go_any.1, bf16[512,2048]{1,0:T(8,128)(2,1)} %w_any.1, bf16[512,512]{1,0:T(8,128)(2,1)} %wo_any.1, s32[1,512]{1,0:T(1,128)} %place.3, s32[1,32]{1,0:T(1,128)} %cnt.1, s32[1,512]{1,0:T(1,128)} %users.1), custom_call_target="tpu_custom_call" | custom-call | tf_op jit(solution)/shard_map/layer/pallas_call | solution.py:539
  80.1 0.0 copy-done.2
  80.1 0.0 copy-start
  80.1 1.2 %copy-done = bf16[32,32,512]{2,1,0:T(8,128)(2,1)S(1)} copy-done((bf16[32,32,512]{2,1,0:T(8,128)(2,1)S(1)}, bf16[32,32,512]{2,1,0:T(8,128)(2,1)}, u32[]{:S(2)}) %copy-start) | copy-done | bytes 1048600
  81.4 0.0 copy-start.1
  81.4 0.9 %copy-done.1 = bf16[8,80,128]{2,1,0:T(8,128)(2,1)S(1)} copy-done((bf16[8,80,128]{2,1,0:T(8,128)(2,1)S(1)}, bf16[8,80,128]{2,1,0:T(8,128)(2,1)}, u32[]{:S(2)}) %copy-start.1) | copy-done | bytes 163864
  82.3 1.5 %finish.1 = (bf16[512,512]{1,0:T(8,128)(2,1)}, f32[64,512]{1,0:T(8,128)}, f32[16,512]{1,0:T(8,128)}) custom-call(bf16[32,32,512]{2,1,0:T(8,128)(2,1)S(1)} %copy-done, bf16[8,80,128]{2,1,0:T(8,128)(2,1)S(1)} %copy-done.1, s32[1,512]{1,0:T(1,128)S(1)} %copy-done.2), custom_call_target="tpu_custom_call" | custom-call | tf_op jit(solution)/shard_map/finish/pallas_call | solution.py:553
Async XLA Ops:
  0.6 79.5 %copy-start.2 = (s32[1,512]{1,0:T(1,128)S(1)}, s32[1,512]{1,0:T(1,128)}, u32[]{:S(2)}) copy-start(s32[1,512]{1,0:T(1,128)} %place.3) | copy-start | bytes 6148
  80.1 1.2 %copy-start = (bf16[32,32,512]{2,1,0:T(8,128)(2,1)S(1)}, bf16[32,32,512]{2,1,0:T(8,128)(2,1)}, u32[]{:S(2)}) copy-start(bf16[32,32,512]{2,1,0:T(8,128)(2,1)} %get-tuple-element.8.ret) | copy-start | bytes 3145732
  81.4 0.9 %copy-start.1 = (bf16[8,80,128]{2,1,0:T(8,128)(2,1)S(1)}, bf16[8,80,128]{2,1,0:T(8,128)(2,1)}, u32[]{:S(2)}) copy-start(bf16[8,80,128]{2,1,0:T(8,128)(2,1)} %get-tuple-element.9.r4) | copy-start | bytes 491524

commit v3 on v2

--- a/solution.py
+++ b/solution.py
@@ -81,54 +81,52 @@
         body(column + lax.rem(inner + j, 8))
 
 
+def drain(ref, sem):
+    pltpu.make_async_copy(ref, ref, sem).wait()
+
+
 class Exchange:
-    def __init__(self, at, src, dst, send, recv, local, whole=False):
+    def __init__(self, at, src, dst, send, recv, whole=False):
         self.at, self.src, self.dst = at, src, dst
-        self.sems, self.local, self.whole = (send, recv), local, whole
+        self.send, self.recv, self.whole = send, recv, whole
 
     def block(self, peer):
         return self.src if self.whole else self.src.at[peer]
 
+    def to(self, peer):
+        at = self.at
+        remote(self.block(peer), self.dst.at[at.me], self.send, self.recv, peer, at.rep).start()
+
     def own(self):
         me = self.at.me
-        return pltpu.make_async_copy(self.block(me), self.dst.at[me], self.local)
-
-    def start(self, dx):
-        at, (send, recv) = self.at, self.sems
-
-        def body(peer):
-            remote(
-                self.block(peer), self.dst.at[at.me], send.at[peer], recv.at[at.me], peer, at.rep
-            ).start()
-
-        each_peer(at, dx, body)
-        if dx == 0:
-            self.own().start()
+        pltpu.make_async_copy(self.block(me), self.dst.at[me], self.recv).start()
 
     def start_all(self):
         for dx in (2, 1, 3, 0):
-            self.start(dx)
+            each_peer(self.at, dx, self.to)
+        self.own()
+
+    def start(self, dx, steps):
+        at = self.at
+        column = lax.rem(at.x + dx, 4) * 8
+        for j in steps:
+            if dx == 0 and j == 0:
+                self.own()
+            else:
+                self.to(column + lax.rem(lax.rem(at.me, 8) + j, 8))
 
     def wait(self):
-        at, (send, recv) = self.at, self.sems
-
-        def body(peer):
-            remote(
-                self.block(peer), self.dst.at[peer], send.at[peer], recv.at[peer], peer, at.rep
-            ).wait()
-
-        for dx in (0, 1, 3, 2):
-            each_peer(at, dx, body)
-        self.own().wait()
+        drain(self.dst, self.recv)
+        drain(self.dst.at[pl.ds(0, DP - 1)], self.send)
 
 
 class Reduce:
-    def __init__(self, at, g, r1, s1, r2, s2, r3, r3w, s3, r4, sems):
+    def __init__(self, at, refs, sems):
         self.at = at
-        self.g, self.r1, self.s1, self.r2, self.s2 = g, r1, s1, r2, s2
-        self.r3, self.r3w, self.s3, self.r4 = r3, r3w, s3, r4
-        (self.a_s, self.a_r, self.b_s, self.b_r, self.c_s, self.c_r,
-         self.w_s, self.w_r, self.d_s, self.d_r) = sems
+        (self.g, self.r1, self.s1, self.r2, self.s2, self.r2x, self.s2x, self.r2y, self.s3x,
+         self.r3, self.r3z, self.r3w, self.s3, self.r4) = refs
+        (self.a_s, self.a_r, self.b_s, self.b_r, self.x_s, self.x_r, self.y_s, self.y_r,
+         self.z_s, self.z_r, self.c_s, self.c_r, self.w_s, self.w_r, self.d_s, self.d_r) = sems
 
     def pair(self, s):
         at = self.at
@@ -136,96 +134,134 @@
             self.g.at[1 - at.core, s], self.r1.at[s], self.a_s.at[s], self.a_r.at[s], at.partner, at.rep
         )
 
-    def over_y(self, s, i):
-        at = self.at
-        y = lax.rem(at.rep + i, REP)
-        return remote(
-            self.s1.at[s, y], self.r2.at[s, i], self.b_s.at[s, i], self.b_r.at[s, i], at.me, y
-        )
-
     def pair_done(self, s):
         at = self.at
         self.pair(s).wait()
         self.s1[s] = (self.g[at.core, s].astype(F32) + self.r1[s].astype(F32)).astype(BF16)
         for i in (2, 1, 3):
-            self.over_y(s, i).start()
+            if s in (1, 2):
+                x = lax.rem(at.x + i, 4)
+                remote(
+                    self.s1.at[s, :, pl.ds(pl.multiple_of(64 * x, 64), 64)], self.r2x.at[s - 1, i],
+                    self.x_s.at[s - 1], self.x_r.at[s - 1], x * 8 + lax.rem(at.me, 8), at.rep,
+                ).start()
+            else:
+                y = lax.rem(at.rep + i, REP)
+                remote(
+                    self.s1.at[s, y], self.r2.at[s, i], self.b_s.at[s], self.b_r.at[s], at.me, y
+                ).start()
 
     def y_done(self, s):
-        for i in (2, 1, 3):
-            self.over_y(s, i).wait()
+        drain(self.r2.at[s, pl.ds(1, 3)], self.b_r.at[s])
+        drain(self.r2.at[s, pl.ds(1, 3)], self.b_s.at[s])
         total = self.s1[s, self.at.rep].astype(F32)
         for i in (1, 2, 3):
             total = total + self.r2[s, i].astype(F32)
         self.s2[s] = total.astype(BF16)
 
-    def column(self, p, x, slot):
-        at = self.at
-        to = x * 4 + p
-        return remote(
-            self.s2.at[1 + p, pl.ds(64 * x, 64)], self.r3.at[slot],
-            self.c_s.at[p, x], self.c_r.at[slot], to * 2 + at.core, at.rep,
-        )
+    def x_done(self, p):
+        at = self.at
+        drain(self.r2x.at[p, pl.ds(1, 3)], self.x_r.at[p])
+        drain(self.r2x.at[p, pl.ds(1, 3)], self.x_s.at[p])
+        total = self.s1[1 + p, :, pl.ds(pl.multiple_of(64 * at.x, 64), 64)].astype(F32)
+        for i in (1, 2, 3):
+            total = total + self.r2x[p, i].astype(F32)
+        self.s2x[p] = total.astype(BF16)
+        for i in (2, 1, 3):
+            y = lax.rem(at.rep + i, REP)
+            remote(
+                self.s2x.at[p, y], self.r2y.at[p, i], self.y_s.at[p], self.y_r.at[p], at.me, y
+            ).start()
+
+    def xy_done(self, p):
+        at = self.at
+        drain(self.r2y.at[p, pl.ds(1, 3)], self.y_r.at[p])
+        drain(self.r2y.at[p, pl.ds(1, 3)], self.y_s.at[p])
+        total = self.s2x[p, at.rep].astype(F32)
+        for i in (1, 2, 3):
+            total = total + self.r2y[p, i].astype(F32)
+        self.s3x[p] = total.astype(BF16)
+
+        @pl.when(at.z != p)
+        def _():
+            to = at.x * 4 + p
+            remote(
+                self.s3x.at[p], self.r3z.at[at.z], self.z_s.at[p], self.z_r, to * 2 + at.core, at.rep
+            ).start()
 
     def columns_start(self, p):
         at = self.at
-        for x in range(4):
-
-            @pl.when(x * 4 + p != at.chip)
-            def _():
-                self.column(p, x, at.chip).start()
-
-    def out_rows(self, other, slot):
-        at = self.at
-        return remote(
-            self.s2.at[0, pl.ds(pl.multiple_of(16 * other, 16), 16)], self.r3w.at[slot],
-            self.w_s.at[other], self.w_r.at[slot], other * 2 + at.core, at.rep,
-        )
+        for x in (2, 1, 3, 0):
+            to = x * 4 + p
+
+            @pl.when(to != at.chip)
+            def _(x=x, to=to):
+                remote(
+                    self.s2.at[1 + p, pl.ds(64 * x, 64)], self.r3.at[at.chip], self.c_s, self.c_r,
+                    to * 2 + at.core, at.rep,
+                ).start()
 
     def out_start(self):
-        @pl.loop(1, CHIPS)
-        def _(i):
-            self.out_rows(lax.rem(self.at.chip + i, CHIPS), self.at.chip).start()
-
-    def gather(self, i, other_core, mine):
-        at = self.at
-        y = lax.rem(at.rep + i, REP)
-        core = 1 - at.core if other_core else at.core
-        slot = at.rep * 2 + at.core if mine else y * 2 + core
-        return remote(
-            self.s3, self.r4.at[slot], self.d_s.at[y * 2 + core], self.d_r.at[slot], at.chip * 2 + core, y
-        )
-
-    def finish(self):
         at = self.at
 
         @pl.loop(1, CHIPS)
         def _(i):
             other = lax.rem(at.chip + i, CHIPS)
-            self.out_rows(other, other).wait()
             remote(
-                self.r3.at[other], self.r3.at[other], self.d_s.at[0], self.c_r.at[other], other * 2 + at.core, at.rep
-            ).wait_recv()
-
-        for p in range(4):
-            for x in range(4):
-
-                @pl.when(x * 4 + p != at.chip)
-                def _(p=p, x=x):
-                    self.column(p, x, at.chip).wait_send()
-
-        self.r3[at.chip] = self.s2[1 + at.z, pl.ds(pl.multiple_of(64 * at.x, 64), 64)]
+                self.s2.at[0, pl.ds(pl.multiple_of(16 * other, 16), 16)], self.r3w.at[at.chip],
+                self.w_s, self.w_r, other * 2 + at.core, at.rep,
+            ).start()
+
+    def total(self, ref, count, rows):
+        total = ref[0].astype(F32)
+        for i in range(1, count):
+            total = total + ref[i].astype(F32)
+        self.s3[rows] = total.astype(BF16)
+
+    def finish(self):
+        at = self.at
+        drain(self.r3w.at[pl.ds(0, CHIPS - 1)], self.w_r)
+        drain(self.r3w.at[pl.ds(0, CHIPS - 1)], self.w_s)
         self.r3w[at.chip] = self.s2[0, pl.ds(pl.multiple_of(16 * at.chip, 16), 16)]
-        for ref, rows in ((self.r3, slice(0, 64)), (self.r3w, slice(64, 80))):
-            total = ref[0].astype(F32)
-            for i in range(1, CHIPS):
-                total = total + ref[i].astype(F32)
-            self.s3[rows] = total.astype(BF16)
-        order = [(i, other) for i in (2, 1, 3, 0) for other in (True, False) if i or other]
-        for i, other in order:
-            self.gather(i, other, True).start()
-        self.r4[at.rep * 2 + at.core] = self.s3[...]
-        for i, other in order:
-            self.gather(i, other, False).wait()
+        self.total(self.r3w, CHIPS, slice(64, 80))
+
+        @pl.when(at.z < 2)
+        def _():
+            drain(self.r3z.at[pl.ds(0, 3)], self.z_r)
+            self.r3z[at.z] = self.s3x[at.z]
+            self.total(self.r3z, 4, slice(0, 64))
+
+        @pl.when(at.z >= 2)
+        def _():
+            drain(self.r3.at[pl.ds(0, CHIPS - 1)], self.c_r)
+            self.r3[at.chip] = self.s2[1 + at.z, pl.ds(pl.multiple_of(64 * at.x, 64), 64)]
+            self.total(self.r3, CHIPS, slice(0, 64))
+
+        for i in (2, 1, 3, 0):
+            for core in (1 - at.core, at.core):
+                if i or core is not at.core:
+                    y = lax.rem(at.rep + i, REP)
+                    remote(
+                        self.s3, self.r4.at[at.rep * 2 + at.core], self.d_s, self.d_r, at.chip * 2 + core, y
+                    ).start()
+        pltpu.make_async_copy(self.s3, self.r4.at[at.rep * 2 + at.core], self.d_r).start()
+        for p in range(2):
+
+            @pl.when(at.z != p)
+            def _(p=p):
+                drain(self.s3x.at[p], self.z_s.at[p])
+
+        @pl.when(at.z < 2)
+        def _():
+            drain(self.r3.at[pl.ds(0, 8)], self.c_s)
+
+        @pl.when(at.z >= 2)
+        def _():
+            drain(self.r3.at[pl.ds(0, 7)], self.c_s)
+
+    def end(self):
+        drain(self.r4, self.d_r)
+        drain(self.r4.at[pl.ds(0, 7)], self.d_s)
 
 
 def slot_positions(ct):
@@ -345,17 +381,26 @@
     dpre[p, :, V] = dv.astype(BF16) * slope[p, :, V]
 
 
-def gate_grad(att, act, slope, dy, wo, da, dpre, gated):
+def gate(att, scale, act, gated):
     for t in range(2):
         rows = slice(256 * t, 256 * t + 256)
-        normed, scale = centred(att[rows])
+        normed, by = centred(att[rows])
         u = jnp.concatenate([act[p, rows, U] for p in range(4)], axis=1).astype(F32)
         gated[rows] = (normed * u).astype(BF16)
+        att[rows] = normed
+        scale[rows] = jnp.broadcast_to(by, (256, 128))
+
+
+def gate_grad(att, scale, act, slope, dy, wo, da, dpre):
+    for t in range(2):
+        rows = slice(256 * t, 256 * t + 256)
+        normed = att[rows]
+        u = jnp.concatenate([act[p, rows, U] for p in range(4)], axis=1).astype(F32)
         dg = dot_nt(dy[rows], wo[...]).astype(BF16).astype(F32)
         du = (dg * normed).astype(BF16)
         for p in range(4):
             dpre[p, rows, U] = du[:, 128 * p : 128 * p + 128] * slope[p, rows, U]
-        da[rows] = norm_grad(dg * u, normed, scale).astype(BF16)
+        da[rows] = norm_grad(dg * u, normed, scale[rows, 0:1]).astype(BF16)
 
 
 def out_grad(dy, gated, g):
@@ -399,56 +444,63 @@
 
 
 def layer_kernel(
-    ev_any, go_any, w_any, wo_any, place, cnt, users,
+    ev_any, go_any, w_any, wo_any, place_any, cnt_any, users_any,
     ret, r4,
-    ev, go, wp, wo, sx, sy, rx, ry, ct, dxp,
-    x, dy, xh, xht, act, slope, mask, wt, gs, att, da, dpre, gated, dx, column,
-    g, r1, s1, r2, s2, r3, r3w, s3,
-    xs, xr, ys, yr, cs, cr, bs, br, loc, load,
-    a_s, a_r, b_s, b_r, c_s, c_r, w_s, w_r, d_s, d_r,
+    place, cnt, users, ev, go, wp, wo, sx, sy, rx, ry, ct, dxp,
+    x, dy, xh, xht, act, slope, mask, wt, gs, att, scale, da, dpre, gated, dx, column,
+    g, r1, s1, r2, s2, r2x, s2x, r2y, s3x, r3, r3z, r3w, s3,
+    load, xs, xr, ys, yr, cs, cr, bs, br, *sems,
 ):
     at = Place()
     barrier = pltpu.get_barrier_semaphore()
-    for dxo in range(4):
+    small = [
+        pltpu.make_async_copy(place_any, place, load.at[0]),
+        pltpu.make_async_copy(ev_any, ev, load.at[1]),
+        pltpu.make_async_copy(cnt_any, cnt, load.at[2]),
+        pltpu.make_async_copy(users_any, users, load.at[3]),
+        pltpu.make_async_copy(go_any, go, load.at[4]),
+        pltpu.make_async_copy(wo_any, wo, load.at[5]),
+    ]
+    small[0].start()
+    small[1].start()
+    for dxo in (2, 1, 3, 0):
         each_peer(at, dxo, lambda peer: signal(barrier, peer, at.rep))
     for i in range(1, REP):
         for c in range(2):
             signal(barrier, at.chip * 2 + c, lax.rem(at.rep + i, REP))
-    loads = [pltpu.make_async_copy(ev_any, ev, load.at[0]), pltpu.make_async_copy(go_any, go, load.at[1])]
+    for copy in small[2:]:
+        copy.start()
     for p in range(4):
         for i in range(4):
-            loads.append(
-                pltpu.make_async_copy(
-                    w_any.at[:, pl.ds(512 * i + 128 * p, 128)],
-                    wp.at[p, :, pl.ds(128 * i, 128)],
-                    load.at[2 + 4 * p + i],
-                )
-            )
-    loads.append(pltpu.make_async_copy(wo_any, wo, load.at[18]))
-    for copy in loads:
-        copy.start()
-    loads[0].wait()
+            pltpu.make_async_copy(
+                w_any.at[:, pl.ds(512 * i + 128 * p, 128)],
+                wp.at[p, :, pl.ds(128 * i, 128)],
+                load.at[6],
+            ).start()
+    small[0].wait()
+    small[1].wait()
     pack(place[...], ev[...], sx)
-    to_x = Exchange(at, sx, rx, xs, xr, loc.at[0])
-    to_y = Exchange(at, sy, ry, ys, yr, loc.at[1])
-    counts = Exchange(at, cnt, ct, cs, cr, loc.at[2], whole=True)
-    back = Exchange(at, dxp, ret, bs, br, loc.at[3])
+    to_x = Exchange(at, sx, rx, xs, xr)
+    to_y = Exchange(at, sy, ry, ys, yr)
+    counts = Exchange(at, cnt, ct, cs, cr, whole=True)
+    back = Exchange(at, dxp, ret, bs, br)
     reduce = Reduce(
-        at, g, r1, s1, r2, s2, r3, r3w, s3, r4,
-        (a_s, a_r, b_s, b_r, c_s, c_r, w_s, w_r, d_s, d_r),
+        at, (g, r1, s1, r2, s2, r2x, s2x, r2y, s3x, r3, r3z, r3w, s3, r4), sems
     )
+    small[2].wait()
     pl.semaphore_wait(barrier, DP - 1 + 2 * (REP - 1))
     counts.start_all()
     to_x.start_all()
-    loads[1].wait()
+    small[4].wait()
     pack(place[...], go[...], sy)
     to_y.start_all()
+    small[3].wait()
     allowed_mask(users, mask)
     counts.wait()
     pos = slot_positions(ct)
     column[...] = column_of(pos, SLOTS)
-    for copy in loads[2:]:
-        copy.wait()
+    small[5].wait()
+    drain(wp, load.at[6])
     to_x.wait()
     compact(pos, rx, x)
     xh[...] = centred(x[...].astype(F32))[0].astype(BF16)
@@ -458,48 +510,64 @@
     def _(p):
         pair_forward(p, xh, wp, mask, act, slope, wt, gs, att)
 
+    gate(att, scale, act, gated)
     to_y.wait()
     compact(pos, ry, dy)
-    gate_grad(att, act, slope, dy, wo, da, dpre, gated)
+    gate_grad(att, scale, act, slope, dy, wo, da, dpre)
     out_grad(dy, gated, g)
     reduce.pair(0).start()
-
-    @pl.loop(0, 4)
-    def _(p):
+    for p in range(4):
         pair_backward(p, act, slope, wt, gs, da, dpre)
         pair_in_grad(p, xht, dpre, g)
         reduce.pair(1 + p).start()
         reduce.pair_done(p)
-
-        @pl.when(p >= 1)
-        def _():
-            reduce.y_done(p - 1)
-
-    reduce.out_start()
-    for p in range(2):
-        reduce.columns_start(p)
     row_grad(x, dy, dpre, wp, dx)
-    reduce.pair_done(4)
+    steps = {
+        2: lambda: reduce.pair_done(4),
+        1: lambda: (reduce.y_done(0), reduce.out_start()),
+        3: lambda: reduce.x_done(0),
+        0: lambda: reduce.x_done(1),
+    }
+    for dxo in (2, 1, 3, 0):
+        spread(lax.rem(at.x + dxo, 4), column, dx, dxp)
+        back.start(dxo, (0, 2, 4, 6))
+        steps[dxo]()
     reduce.y_done(3)
     reduce.columns_start(2)
-    for dxo in (2, 1, 3):
-        spread(lax.rem(at.x + dxo, 4), column, dx, dxp)
-        back.start(dxo)
-    spread(at.x, column, dx, dxp)
+    reduce.xy_done(0)
+    reduce.xy_done(1)
+    for dxo in (2, 1, 3, 0):
+        back.start(dxo, (1, 5))
     reduce.y_done(4)
     reduce.columns_start(3)
-    back.start(0)
+    for dxo in (2, 1, 3, 0):
+        back.start(dxo, (3, 7))
     reduce.finish()
+    reduce.end()
     back.wait()
 
 
-def finish_kernel(ret, r4, place, ge, gw, gout):
+def finish_kernel(ret_any, r4_any, place, ge, gw, gout, ret, r4, sems):
+    parts = [
+        pltpu.make_async_copy(ret_any.at[pl.ds(8 * i, 8)], ret.at[pl.ds(8 * i, 8)], sems.at[i])
+        for i in range(4)
+    ]
+    sums = pltpu.make_async_copy(r4_any, r4, sems.at[4])
+    for copy in (*parts, sums):
+        copy.start()
     core = lax.rem(lax.axis_index("dp"), 2)
     column = column_of(place[...].astype(F32), N)
-    hot = jnp.concatenate(
-        [onehot((iota((N, 128), 1) + 128 * b).astype(F32) == column) for b in range(8)], axis=1
-    )
-    ge[...] = dot(hot, ret[...].reshape(SLOTS, N)).astype(BF16)
+    total = None
+    for i in range(4):
+        hot = jnp.concatenate(
+            [onehot((iota((N, 128), 1) + 256 * i + 128 * b).astype(F32) == column) for b in range(2)],
+            axis=1,
+        )
+        parts[i].wait()
+        part = dot(hot, ret[8 * i : 8 * i + 8].reshape(256, N))
+        total = part if total is None else total + part
+    ge[...] = total.astype(BF16)
+    sums.wait()
     for c in range(2):
         for half in range(2):
             block = jnp.concatenate([r4[4 * half + c, :64], r4[4 * half + 2 + c, :64]], axis=0)
@@ -515,21 +583,26 @@
 SQUARE = pltpu.VMEM((N, N), BF16)
 PAIRS = pltpu.VMEM((4, N, N), BF16)
 TERMS = pltpu.VMEM((5, 4, 256, 128), BF16)
+COLUMNS = pltpu.VMEM((2, 4, 64, 128), BF16)
 SCRATCH = [
+    pltpu.VMEM((1, N), I32), pltpu.VMEM((1, DP), I32), pltpu.VMEM((1, N), I32),
     SQUARE, SQUARE, PAIRS, SQUARE,
     BLOCKS, BLOCKS, BLOCKS, BLOCKS, pltpu.VMEM((DP, 1, DP), I32), BLOCKS,
     SQUARE, SQUARE, SQUARE, SQUARE, PAIRS, PAIRS, SQUARE,
     pltpu.VMEM((HEADS, N, N), BF16), pltpu.VMEM((HEADS, N, N), BF16),
-    pltpu.VMEM((N, N), F32), SQUARE, PAIRS, SQUARE, SQUARE,
+    pltpu.VMEM((N, N), F32), pltpu.VMEM((N, 128), F32),
+    SQUARE, PAIRS, SQUARE, SQUARE,
     pltpu.VMEM((SLOTS, 128), F32),
     pltpu.VMEM((2, 5, 4, 256, 128), BF16), TERMS, TERMS, TERMS,
     pltpu.VMEM((5, 256, 128), BF16),
-    pltpu.VMEM((CHIPS, 64, 128), BF16), pltpu.VMEM((CHIPS, 16, 128), BF16),
-    pltpu.VMEM((80, 128), BF16),
-    DMA((DP,)), DMA((DP,)), DMA((DP,)), DMA((DP,)), DMA((DP,)), DMA((DP,)), DMA((DP,)), DMA((DP,)),
-    DMA((4,)), DMA((19,)),
-    DMA((5,)), DMA((5,)), DMA((5, 4)), DMA((5, 4)), DMA((4, 4)), DMA((CHIPS,)),
-    DMA((CHIPS,)), DMA((CHIPS,)), DMA((8,)), DMA((8,)),
+    pltpu.VMEM((2, 4, 4, 64, 128), BF16), COLUMNS, COLUMNS,
+    pltpu.VMEM((2, 64, 128), BF16),
+    pltpu.VMEM((CHIPS, 64, 128), BF16), pltpu.VMEM((4, 64, 128), BF16),
+    pltpu.VMEM((CHIPS, 16, 128), BF16), pltpu.VMEM((80, 128), BF16),
+    DMA((7,)), DMA, DMA, DMA, DMA, DMA, DMA, DMA, DMA,
+    DMA((5,)), DMA((5,)), DMA((5,)), DMA((5,)),
+    DMA((2,)), DMA((2,)), DMA((2,)), DMA((2,)), DMA((2,)), DMA,
+    DMA, DMA, DMA, DMA, DMA, DMA,
 ]
 VM = pl.BlockSpec(memory_space=pltpu.VMEM)
 ANY = pl.BlockSpec(memory_space=pl.ANY)
@@ -543,8 +616,8 @@
             jax.ShapeDtypeStruct((DP, CAP, N), BF16),
             jax.ShapeDtypeStruct((8, 80, 128), BF16),
         ),
-        in_specs=[ANY] * 4 + [VM] * 3,
-        out_specs=(VM,) * 2,
+        in_specs=[ANY] * 7,
+        out_specs=(ANY,) * 2,
         scratch_shapes=SCRATCH,
         compiler_params=pltpu.CompilerParams(
             collective_id=0, has_side_effects=True, vmem_limit_bytes=VMEM_LIMIT
@@ -558,9 +631,10 @@
             jax.ShapeDtypeStruct((64, N), F32),
             jax.ShapeDtypeStruct((16, N), F32),
         ),
-        in_specs=[VM] * 3,
+        in_specs=[ANY, ANY, VM],
         out_specs=(VM,) * 3,
-        compiler_params=pltpu.CompilerParams(vmem_limit_bytes=32 * 1024 * 1024),
+        scratch_shapes=[BLOCKS, pltpu.VMEM((8, 80, 128), BF16), DMA((5,))],
+        compiler_params=pltpu.CompilerParams(vmem_limit_bytes=VMEM_LIMIT),
     )(ret, r4, send_place)
     return ge, gw.T, gout.T
 

time: 84 us -> 71.3 us (0.85)
  Pallas kernels: 81 us -> 70 us
  local copies, waits for them, and re-layouts: 2.14 us -> 0 us
    pallas_call x1, Pallas kernels: 79.5 us -> 66.6 us  [on_device(): pl.pallas_call(layer_kernel, name='layer', out_shape=(jax.ShapeDtypeStruc...]
    unnamed x6 -> x0, local copies, waits for them, and re-layouts: 2.14 us -> none
    pallas_call x1, Pallas kernels: 1.55 us -> 3.4 us  [on_device(): pl.pallas_call(finish_kernel, name='finish', out_shape=(jax.ShapeDtypeStr...]
where the time goes in v3:
time: 71.3 us; the launch traced here: 70.8 us
  Pallas kernels  70 us (98%)
  between operations  0.8 us (1%)
    pallas_call x1, Pallas kernels, on_device(): pl.pallas_call(layer_kernel, name='layer', out_shape=(jax.ShapeDtypeStruc...  66.6 us
    pallas_call x1, Pallas kernels, on_device(): pl.pallas_call(finish_kernel, name='finish', out_shape=(jax.ShapeDtypeStr...  3.4 us

profile of v3, /device:TPU:96, one launch (start us, length us, event | category | flops | bytes accessed | tf_op | source)
XLA Modules:
  0.0 70.8 jit_solution(13562199928393009471)
XLA Ops:
  0.6 66.6 %layer.1 = (bf16[32,32,512]{2,1,0:T(8,128)(2,1)}, bf16[8,80,128]{2,1,0:T(8,128)(2,1)}) custom-call(bf16[512,512]{1,0:T(8,128)(2,1)} %ev_any.1, bf16[512,512]{1,0:T(8,128)(2,1)} %go_any.1, bf16[512,2048]{1,0:T(8,128)(2,1)} %w_any.1, bf16[512,512]{1,0:T(8,128)(2,1)} %wo_any.1, s32[1,512]{1,0:T(1,128)} %place.1, s32[1,32]{1,0:T(1,128)} %cnt_any.1, ...), custom_call_target="tpu_custom_call" | custom-call | tf_op jit(solution)/shard_map/layer/pallas_call | solution.py:612
  67.3 3.4 %finish.1 = (bf16[512,512]{1,0:T(8,128)(2,1)}, f32[64,512]{1,0:T(8,128)}, f32[16,512]{1,0:T(8,128)}) custom-call(bf16[32,32,512]{2,1,0:T(8,128)(2,1)} %get-tuple-element.8.ret_any, bf16[8,80,128]{2,1,0:T(8,128)(2,1)} %get-tuple-element.9.r4_any, s32[1,512]{1,0:T(1,128)} %place.1), custom_call_target="tpu_custom_call" | custom-call | tf_op jit(solution)/shard_map/finish/pallas_call | solution.py:626

commit v4 on v3

--- a/solution.py
+++ b/solution.py
@@ -66,10 +66,9 @@
         self.partner = self.chip * 2 + (1 - self.core)
 
 
-def pack(place, rows, out):
-    for chunk in range(4):
-        hot = onehot(iota((256, N), 0) + 256 * chunk == place)
-        out[8 * chunk : 8 * chunk + 8] = dot(hot, rows).astype(BF16).reshape(8, CAP, N)
+def pack(chunk, place, rows, out):
+    hot = onehot(iota((256, N), 0) + 256 * chunk == place[...])
+    out[pl.ds(8 * chunk, 8)] = dot(hot, rows[...]).astype(BF16).reshape(8, CAP, N)
 
 
 def each_peer(at, dx, body):
@@ -101,10 +100,10 @@
         me = self.at.me
         pltpu.make_async_copy(self.block(me), self.dst.at[me], self.recv).start()
 
-    def start_all(self):
-        for dx in (2, 1, 3, 0):
-            each_peer(self.at, dx, self.to)
-        self.own()
+    def start_column(self, dx):
+        each_peer(self.at, dx, self.to)
+        if dx == 0:
+            self.own()
 
     def start(self, dx, steps):
         at = self.at
@@ -124,9 +123,10 @@
     def __init__(self, at, refs, sems):
         self.at = at
         (self.g, self.r1, self.s1, self.r2, self.s2, self.r2x, self.s2x, self.r2y, self.s3x,
-         self.r3, self.r3z, self.r3w, self.s3, self.r4) = refs
+         self.r5, self.r3z, self.rwx, self.s2w, self.rwy, self.s3, self.r4) = refs
         (self.a_s, self.a_r, self.b_s, self.b_r, self.x_s, self.x_r, self.y_s, self.y_r,
-         self.z_s, self.z_r, self.c_s, self.c_r, self.w_s, self.w_r, self.d_s, self.d_r) = sems
+         self.z_s, self.z_r, self.e_s, self.e_r, self.w_s, self.w_r, self.v_s, self.v_r,
+         self.d_s, self.d_r) = sems
 
     def pair(self, s):
         at = self.at
@@ -139,47 +139,47 @@
         self.pair(s).wait()
         self.s1[s] = (self.g[at.core, s].astype(F32) + self.r1[s].astype(F32)).astype(BF16)
         for i in (2, 1, 3):
-            if s in (1, 2):
-                x = lax.rem(at.x + i, 4)
-                remote(
-                    self.s1.at[s, :, pl.ds(pl.multiple_of(64 * x, 64), 64)], self.r2x.at[s - 1, i],
-                    self.x_s.at[s - 1], self.x_r.at[s - 1], x * 8 + lax.rem(at.me, 8), at.rep,
-                ).start()
-            else:
+            if s in (2, 4):
                 y = lax.rem(at.rep + i, REP)
                 remote(
                     self.s1.at[s, y], self.r2.at[s, i], self.b_s.at[s], self.b_r.at[s], at.me, y
                 ).start()
+                continue
+            t = 2 if s == 0 else s // 2
+            other = lax.rem((at.z if s == 0 else at.x) + i, 4)
+            to = at.x * 8 + other * 2 + at.core if s == 0 else other * 8 + lax.rem(at.me, 8)
+            remote(
+                self.s1.at[s, :, pl.ds(pl.multiple_of(64 * other, 64), 64)], self.r2x.at[t, i],
+                self.x_s.at[t], self.x_r.at[t], to, at.rep,
+            ).start()
 
     def y_done(self, s):
+        at = self.at
         drain(self.r2.at[s, pl.ds(1, 3)], self.b_r.at[s])
         drain(self.r2.at[s, pl.ds(1, 3)], self.b_s.at[s])
         total = self.s1[s, self.at.rep].astype(F32)
         for i in (1, 2, 3):
             total = total + self.r2[s, i].astype(F32)
         self.s2[s] = total.astype(BF16)
-
-    def x_done(self, p):
-        at = self.at
-        drain(self.r2x.at[p, pl.ds(1, 3)], self.x_r.at[p])
-        drain(self.r2x.at[p, pl.ds(1, 3)], self.x_s.at[p])
-        total = self.s1[1 + p, :, pl.ds(pl.multiple_of(64 * at.x, 64), 64)].astype(F32)
+        u = s // 2 - 1
+        for i in (2, 1, 3):
+            x = lax.rem(at.x + i, 4)
+            remote(
+                self.s2.at[s, pl.ds(pl.multiple_of(64 * x, 64), 64)], self.r5.at[u, i],
+                self.e_s.at[u], self.e_r.at[u], x * 8 + lax.rem(at.me, 8), at.rep,
+            ).start()
+
+    def yx_done(self, s):
+        u = s // 2 - 1
+        drain(self.r5.at[u, pl.ds(1, 3)], self.e_r.at[u])
+        drain(self.r5.at[u, pl.ds(1, 3)], self.e_s.at[u])
+        total = self.s2[s, pl.ds(pl.multiple_of(64 * self.at.x, 64), 64)].astype(F32)
         for i in (1, 2, 3):
-            total = total + self.r2x[p, i].astype(F32)
-        self.s2x[p] = total.astype(BF16)
-        for i in (2, 1, 3):
-            y = lax.rem(at.rep + i, REP)
-            remote(
-                self.s2x.at[p, y], self.r2y.at[p, i], self.y_s.at[p], self.y_r.at[p], at.me, y
-            ).start()
-
-    def xy_done(self, p):
-        at = self.at
-        drain(self.r2y.at[p, pl.ds(1, 3)], self.y_r.at[p])
-        drain(self.r2y.at[p, pl.ds(1, 3)], self.y_s.at[p])
-        total = self.s2x[p, at.rep].astype(F32)
-        for i in (1, 2, 3):
-            total = total + self.r2y[p, i].astype(F32)
+            total = total + self.r5[u, i].astype(F32)
+        self.to_z(s - 1, total)
+
+    def to_z(self, p, total):
+        at = self.at
         self.s3x[p] = total.astype(BF16)
 
         @pl.when(at.z != p)
@@ -189,28 +189,54 @@
                 self.s3x.at[p], self.r3z.at[at.z], self.z_s.at[p], self.z_r, to * 2 + at.core, at.rep
             ).start()
 
-    def columns_start(self, p):
-        at = self.at
-        for x in (2, 1, 3, 0):
-            to = x * 4 + p
-
-            @pl.when(to != at.chip)
-            def _(x=x, to=to):
-                remote(
-                    self.s2.at[1 + p, pl.ds(64 * x, 64)], self.r3.at[at.chip], self.c_s, self.c_r,
-                    to * 2 + at.core, at.rep,
-                ).start()
-
-    def out_start(self):
-        at = self.at
-
-        @pl.loop(1, CHIPS)
-        def _(i):
-            other = lax.rem(at.chip + i, CHIPS)
+    def first_sum(self, t):
+        at = self.at
+        s, own = (0, at.z) if t == 2 else (1 + 2 * t, at.x)
+        drain(self.r2x.at[t, pl.ds(1, 3)], self.x_r.at[t])
+        drain(self.r2x.at[t, pl.ds(1, 3)], self.x_s.at[t])
+        total = self.s1[s, :, pl.ds(pl.multiple_of(64 * own, 64), 64)].astype(F32)
+        for i in (1, 2, 3):
+            total = total + self.r2x[t, i].astype(F32)
+        self.s2x[t] = total.astype(BF16)
+
+    def x_done(self, t):
+        at = self.at
+        self.first_sum(t)
+        for i in (2, 1, 3):
+            y = lax.rem(at.rep + i, REP)
             remote(
-                self.s2.at[0, pl.ds(pl.multiple_of(16 * other, 16), 16)], self.r3w.at[at.chip],
-                self.w_s, self.w_r, other * 2 + at.core, at.rep,
+                self.s2x.at[t, y], self.r2y.at[t, i], self.y_s.at[t], self.y_r.at[t], at.me, y
             ).start()
+
+    def xy_done(self, t):
+        drain(self.r2y.at[t, pl.ds(1, 3)], self.y_r.at[t])
+        drain(self.r2y.at[t, pl.ds(1, 3)], self.y_s.at[t])
+        total = self.s2x[t, self.at.rep].astype(F32)
+        for i in (1, 2, 3):
+            total = total + self.r2y[t, i].astype(F32)
+        self.to_z(2 * t, total)
+
+    def out_x_start(self):
+        at = self.at
+        self.first_sum(2)
+        for i in (2, 1, 3):
+            x = lax.rem(at.x + i, 4)
+            remote(
+                self.s2x.at[2, :, pl.ds(pl.multiple_of(16 * x, 16), 16)], self.rwx.at[i],
+                self.w_s, self.w_r, x * 8 + lax.rem(at.me, 8), at.rep,
+            ).start()
+
+    def out_y_start(self):
+        at = self.at
+        drain(self.rwx.at[pl.ds(1, 3)], self.w_r)
+        drain(self.rwx.at[pl.ds(1, 3)], self.w_s)
+        total = self.s2x[2, :, pl.ds(pl.multiple_of(16 * at.x, 16), 16)].astype(F32)
+        for i in (1, 2, 3):
+            total = total + self.rwx[i].astype(F32)
+        self.s2w[...] = total.astype(BF16)
+        for i in (2, 1, 3):
+            y = lax.rem(at.rep + i, REP)
+            remote(self.s2w.at[y], self.rwy.at[i], self.v_s, self.v_r, at.me, y).start()
 
     def total(self, ref, count, rows):
         total = ref[0].astype(F32)
@@ -220,44 +246,26 @@
 
     def finish(self):
         at = self.at
-        drain(self.r3w.at[pl.ds(0, CHIPS - 1)], self.w_r)
-        drain(self.r3w.at[pl.ds(0, CHIPS - 1)], self.w_s)
-        self.r3w[at.chip] = self.s2[0, pl.ds(pl.multiple_of(16 * at.chip, 16), 16)]
-        self.total(self.r3w, CHIPS, slice(64, 80))
-
-        @pl.when(at.z < 2)
-        def _():
-            drain(self.r3z.at[pl.ds(0, 3)], self.z_r)
-            self.r3z[at.z] = self.s3x[at.z]
-            self.total(self.r3z, 4, slice(0, 64))
-
-        @pl.when(at.z >= 2)
-        def _():
-            drain(self.r3.at[pl.ds(0, CHIPS - 1)], self.c_r)
-            self.r3[at.chip] = self.s2[1 + at.z, pl.ds(pl.multiple_of(64 * at.x, 64), 64)]
-            self.total(self.r3, CHIPS, slice(0, 64))
-
+        drain(self.rwy.at[pl.ds(1, 3)], self.v_r)
+        drain(self.rwy.at[pl.ds(1, 3)], self.v_s)
+        self.rwy[0] = self.s2w[at.rep]
+        self.total(self.rwy, 4, slice(64, 80))
+
+        drain(self.r3z.at[pl.ds(0, 3)], self.z_r)
+        self.r3z[at.z] = self.s3x[at.z]
+        self.total(self.r3z, 4, slice(0, 64))
+        mine = self.r4.at[at.rep * 2 + at.core]
         for i in (2, 1, 3, 0):
             for core in (1 - at.core, at.core):
                 if i or core is not at.core:
                     y = lax.rem(at.rep + i, REP)
-                    remote(
-                        self.s3, self.r4.at[at.rep * 2 + at.core], self.d_s, self.d_r, at.chip * 2 + core, y
-                    ).start()
-        pltpu.make_async_copy(self.s3, self.r4.at[at.rep * 2 + at.core], self.d_r).start()
-        for p in range(2):
+                    remote(self.s3, mine, self.d_s, self.d_r, at.chip * 2 + core, y).start()
+        pltpu.make_async_copy(self.s3, mine, self.d_r).start()
+        for p in range(4):
 
             @pl.when(at.z != p)
             def _(p=p):
                 drain(self.s3x.at[p], self.z_s.at[p])
-
-        @pl.when(at.z < 2)
-        def _():
-            drain(self.r3.at[pl.ds(0, 8)], self.c_s)
-
-        @pl.when(at.z >= 2)
-        def _():
-            drain(self.r3.at[pl.ds(0, 7)], self.c_s)
 
     def end(self):
         drain(self.r4, self.d_r)
@@ -280,9 +288,10 @@
 def compact(pos, rows_ref, out_ref):
     rows = rows_ref[...].reshape(SLOTS, N)
     for chunk in range(2):
-        index = (iota((256, SLOTS), 0) + 256 * chunk).astype(F32)
-        hot = onehot(index == pos)
-        out_ref[256 * chunk : 256 * chunk + 256] = dot(hot, rows).astype(BF16)
+        slots = slice(256 * chunk, 256 * chunk + 768)
+        index = (iota((256, 768), 0) + 256 * chunk).astype(F32)
+        hot = onehot(index == pos[:, slots])
+        out_ref[256 * chunk : 256 * chunk + 256] = dot(hot, rows[slots]).astype(BF16)
 
 
 def centred(values):
@@ -405,10 +414,12 @@
 
 def out_grad(dy, gated, g):
     term = dot(jnp.transpose(dy[...]), gated[...]).astype(BF16)
-    term = term.reshape(CHIPS, 2, 16, N)
-    for c in range(2):
-        for y in range(4):
-            g[c, 0, y] = term[:, c, :, 128 * y : 128 * y + 128].reshape(256, 128)
+    for chip in range(CHIPS):
+        first = 64 * (chip % 4) + 16 * (chip // 4)
+        for c in range(2):
+            row = 32 * chip + 16 * c
+            for y in range(4):
+                g[c, 0, y, first : first + 16, :] = term[row : row + 16, 128 * y : 128 * y + 128]
 
 
 def pair_in_grad(p, xht, dpre, g):
@@ -424,15 +435,15 @@
                     ]
 
 
-def row_grad(x, dy, dpre, wp, dx):
+def row_grad(xn, xscale, dy, dpre, wp, dx):
     for t in range(2):
         rows = slice(256 * t, 256 * t + 256)
         dxh = dot_nt(dpre[0, rows], wp[0])
         for p in range(1, 4):
             dxh = dxh + dot_nt(dpre[p, rows], wp[p])
         dxh = dxh.astype(BF16).astype(F32)
-        normed, scale = centred(x[rows].astype(F32))
-        dx[rows] = (norm_grad(dxh, normed, scale) + dy[rows].astype(F32)).astype(BF16)
+        grad = norm_grad(dxh, xn[rows], xscale[rows, 0:1])
+        dx[rows] = (grad + dy[rows].astype(F32)).astype(BF16)
 
 
 def spread(chunk, column, dx, out):
@@ -447,8 +458,8 @@
     ev_any, go_any, w_any, wo_any, place_any, cnt_any, users_any,
     ret, r4,
     place, cnt, users, ev, go, wp, wo, sx, sy, rx, ry, ct, dxp,
-    x, dy, xh, xht, act, slope, mask, wt, gs, att, scale, da, dpre, gated, dx, column,
-    g, r1, s1, r2, s2, r2x, s2x, r2y, s3x, r3, r3z, r3w, s3,
+    x, xn, xscale, dy, xh, xht, act, slope, mask, wt, gs, att, scale, da, dpre, gated, dx, column,
+    g, r1, s1, r2, s2, r2x, s2x, r2y, s3x, r5, r3z, rwx, s2w, rwy, s3,
     load, xs, xr, ys, yr, cs, cr, bs, br, *sems,
 ):
     at = Place()
@@ -479,31 +490,41 @@
             ).start()
     small[0].wait()
     small[1].wait()
-    pack(place[...], ev[...], sx)
     to_x = Exchange(at, sx, rx, xs, xr)
     to_y = Exchange(at, sy, ry, ys, yr)
     counts = Exchange(at, cnt, ct, cs, cr, whole=True)
     back = Exchange(at, dxp, ret, bs, br)
     reduce = Reduce(
-        at, (g, r1, s1, r2, s2, r2x, s2x, r2y, s3x, r3, r3z, r3w, s3, r4), sems
+        at, (g, r1, s1, r2, s2, r2x, s2x, r2y, s3x, r5, r3z, rwx, s2w, rwy, s3, r4), sems
     )
+    columns = (2, 1, 3, 0)
+    pack(lax.rem(at.x + 2, 4), place, ev, sx)
     small[2].wait()
     pl.semaphore_wait(barrier, DP - 1 + 2 * (REP - 1))
-    counts.start_all()
-    to_x.start_all()
+    for dxo in columns:
+        counts.start_column(dxo)
+    to_x.start_column(2)
+    for dxo in (1, 3, 0):
+        pack(lax.rem(at.x + dxo, 4), place, ev, sx)
+        to_x.start_column(dxo)
     small[4].wait()
-    pack(place[...], go[...], sy)
-    to_y.start_all()
+    for dxo in columns:
+        pack(lax.rem(at.x + dxo, 4), place, go, sy)
     small[3].wait()
     allowed_mask(users, mask)
     counts.wait()
+    for dxo in columns:
+        to_y.start_column(dxo)
     pos = slot_positions(ct)
     column[...] = column_of(pos, SLOTS)
     small[5].wait()
     drain(wp, load.at[6])
     to_x.wait()
     compact(pos, rx, x)
-    xh[...] = centred(x[...].astype(F32))[0].astype(BF16)
+    normed, by = centred(x[...].astype(F32))
+    xn[...] = normed
+    xscale[...] = jnp.broadcast_to(by, (N, 128))
+    xh[...] = normed.astype(BF16)
     xht[...] = jnp.transpose(xh[...])
 
     @pl.loop(0, 4)
@@ -521,53 +542,49 @@
         pair_in_grad(p, xht, dpre, g)
         reduce.pair(1 + p).start()
         reduce.pair_done(p)
-    row_grad(x, dy, dpre, wp, dx)
-    steps = {
-        2: lambda: reduce.pair_done(4),
-        1: lambda: (reduce.y_done(0), reduce.out_start()),
-        3: lambda: reduce.x_done(0),
-        0: lambda: reduce.x_done(1),
-    }
-    for dxo in (2, 1, 3, 0):
+    row_grad(xn, xscale, dy, dpre, wp, dx)
+    for dxo in columns:
         spread(lax.rem(at.x + dxo, 4), column, dx, dxp)
-        back.start(dxo, (0, 2, 4, 6))
-        steps[dxo]()
-    reduce.y_done(3)
-    reduce.columns_start(2)
+        back.start(dxo, (0, 2, 4))
+        if dxo == 2:
+            reduce.pair_done(4)
+    reduce.x_done(0)
+    reduce.out_x_start()
+    reduce.y_done(2)
     reduce.xy_done(0)
+    for dxo in columns:
+        back.start(dxo, (6,))
+    reduce.x_done(1)
+    reduce.out_y_start()
+    reduce.y_done(4)
+    for dxo in columns:
+        back.start(dxo, (1, 5))
+    reduce.yx_done(2)
     reduce.xy_done(1)
-    for dxo in (2, 1, 3, 0):
-        back.start(dxo, (1, 5))
-    reduce.y_done(4)
-    reduce.columns_start(3)
-    for dxo in (2, 1, 3, 0):
-        back.start(dxo, (3, 7))
+    for dxo in columns:
+        back.start(dxo, (3,))
+    reduce.yx_done(4)
+    for dxo in columns:
+        back.start(dxo, (7,))
     reduce.finish()
     reduce.end()
     back.wait()
 
 
-def finish_kernel(ret_any, r4_any, place, ge, gw, gout, ret, r4, sems):
-    parts = [
-        pltpu.make_async_copy(ret_any.at[pl.ds(8 * i, 8)], ret.at[pl.ds(8 * i, 8)], sems.at[i])
-        for i in range(4)
-    ]
-    sums = pltpu.make_async_copy(r4_any, r4, sems.at[4])
-    for copy in (*parts, sums):
-        copy.start()
+def finish_kernel(ret, r4, place, ge_any, gw_any, gout_any, ge, gw, gout, sems):
     core = lax.rem(lax.axis_index("dp"), 2)
     column = column_of(place[...].astype(F32), N)
-    total = None
-    for i in range(4):
+    stores = []
+    for t in range(2):
+        rows = slice(256 * t, 256 * t + 256)
         hot = jnp.concatenate(
-            [onehot((iota((N, 128), 1) + 256 * i + 128 * b).astype(F32) == column) for b in range(2)],
+            [onehot((iota((256, 128), 1) + 128 * b).astype(F32) == column[rows]) for b in range(8)],
             axis=1,
         )
-        parts[i].wait()
-        part = dot(hot, ret[8 * i : 8 * i + 8].reshape(256, N))
-        total = part if total is None else total + part
-    ge[...] = total.astype(BF16)
-    sums.wait()
+        ge[rows] = dot(hot, ret[...].reshape(SLOTS, N)).astype(BF16)
+        part = pl.ds(256 * t, 256)
+        stores.append(pltpu.make_async_copy(ge.at[part], ge_any.at[part], sems.at[t]))
+        stores[-1].start()
     for c in range(2):
         for half in range(2):
             block = jnp.concatenate([r4[4 * half + c, :64], r4[4 * half + 2 + c, :64]], axis=0)
@@ -576,6 +593,12 @@
             gw[:, first : first + 128] = jnp.where(core == 1, block[64:], block[:64])
     for y in range(4):
         gout[:, 128 * y : 128 * y + 128] = r4[2 * y + core, 64:80].astype(F32)
+    stores.append(pltpu.make_async_copy(gw, gw_any, sems.at[2]))
+    stores.append(pltpu.make_async_copy(gout, gout_any, sems.at[3]))
+    stores[2].start()
+    stores[3].start()
+    for copy in stores:
+        copy.wait()
 
 
 DMA = pltpu.SemaphoreType.DMA
@@ -588,21 +611,23 @@
     pltpu.VMEM((1, N), I32), pltpu.VMEM((1, DP), I32), pltpu.VMEM((1, N), I32),
     SQUARE, SQUARE, PAIRS, SQUARE,
     BLOCKS, BLOCKS, BLOCKS, BLOCKS, pltpu.VMEM((DP, 1, DP), I32), BLOCKS,
-    SQUARE, SQUARE, SQUARE, SQUARE, PAIRS, PAIRS, SQUARE,
+    SQUARE, pltpu.VMEM((N, N), F32), pltpu.VMEM((N, 128), F32),
+    SQUARE, SQUARE, SQUARE, PAIRS, PAIRS, SQUARE,
     pltpu.VMEM((HEADS, N, N), BF16), pltpu.VMEM((HEADS, N, N), BF16),
     pltpu.VMEM((N, N), F32), pltpu.VMEM((N, 128), F32),
     SQUARE, PAIRS, SQUARE, SQUARE,
     pltpu.VMEM((SLOTS, 128), F32),
     pltpu.VMEM((2, 5, 4, 256, 128), BF16), TERMS, TERMS, TERMS,
     pltpu.VMEM((5, 256, 128), BF16),
-    pltpu.VMEM((2, 4, 4, 64, 128), BF16), COLUMNS, COLUMNS,
-    pltpu.VMEM((2, 64, 128), BF16),
-    pltpu.VMEM((CHIPS, 64, 128), BF16), pltpu.VMEM((4, 64, 128), BF16),
-    pltpu.VMEM((CHIPS, 16, 128), BF16), pltpu.VMEM((80, 128), BF16),
+    pltpu.VMEM((3, 4, 4, 64, 128), BF16), pltpu.VMEM((3, 4, 64, 128), BF16), COLUMNS,
+    pltpu.VMEM((4, 64, 128), BF16),
+    pltpu.VMEM((2, 4, 64, 128), BF16), pltpu.VMEM((4, 64, 128), BF16),
+    pltpu.VMEM((4, 4, 16, 128), BF16), pltpu.VMEM((4, 16, 128), BF16),
+    pltpu.VMEM((4, 16, 128), BF16), pltpu.VMEM((80, 128), BF16),
     DMA((7,)), DMA, DMA, DMA, DMA, DMA, DMA, DMA, DMA,
     DMA((5,)), DMA((5,)), DMA((5,)), DMA((5,)),
-    DMA((2,)), DMA((2,)), DMA((2,)), DMA((2,)), DMA((2,)), DMA,
-    DMA, DMA, DMA, DMA, DMA, DMA,
+    DMA((3,)), DMA((3,)), DMA((2,)), DMA((2,)), DMA((4,)), DMA,
+    DMA((2,)), DMA((2,)), DMA, DMA, DMA, DMA, DMA, DMA,
 ]
 VM = pl.BlockSpec(memory_space=pltpu.VMEM)
 ANY = pl.BlockSpec(memory_space=pl.ANY)
@@ -612,12 +637,9 @@
     ret, r4 = pl.pallas_call(
         layer_kernel,
         name="layer",
-        out_shape=(
-            jax.ShapeDtypeStruct((DP, CAP, N), BF16),
-            jax.ShapeDtypeStruct((8, 80, 128), BF16),
-        ),
+        out_shape=(pltpu.VMEM((DP, CAP, N), BF16), pltpu.VMEM((8, 80, 128), BF16)),
         in_specs=[ANY] * 7,
-        out_specs=(ANY,) * 2,
+        out_specs=(VM,) * 2,
         scratch_shapes=SCRATCH,
         compiler_params=pltpu.CompilerParams(
             collective_id=0, has_side_effects=True, vmem_limit_bytes=VMEM_LIMIT
@@ -631,10 +653,12 @@
             jax.ShapeDtypeStruct((64, N), F32),
             jax.ShapeDtypeStruct((16, N), F32),
         ),
-        in_specs=[ANY, ANY, VM],
-        out_specs=(VM,) * 3,
-        scratch_shapes=[BLOCKS, pltpu.VMEM((8, 80, 128), BF16), DMA((5,))],
-        compiler_params=pltpu.CompilerParams(vmem_limit_bytes=VMEM_LIMIT),
+        in_specs=[VM] * 3,
+        out_specs=(ANY,) * 3,
+        scratch_shapes=[
+            SQUARE, pltpu.VMEM((64, N), F32), pltpu.VMEM((16, N), F32), DMA((4,)),
+        ],
+        compiler_params=pltpu.CompilerParams(vmem_limit_bytes=16 * 1024 * 1024),
     )(ret, r4, send_place)
     return ge, gw.T, gout.T
 

time: 71.3 us -> 67.8 us (0.951)
  Pallas kernels: 70 us -> 66.8 us
    pallas_call x1, Pallas kernels: 3.4 us -> 1.54 us  [on_device(): pl.pallas_call(finish_kernel, name='finish', out_shape=(jax.ShapeDtypeStr...]
    pallas_call x1, Pallas kernels: 66.6 us -> 65.2 us  [on_device(): pl.pallas_call(layer_kernel, name='layer', out_shape=(pltpu.VMEM((DP, CAP...]
where the time goes in v4:
time: 67.8 us; the launch traced here: 67.6 us
  Pallas kernels  66.8 us (99%)
  between operations  0.82 us (1%)
    pallas_call x1, Pallas kernels, on_device(): pl.pallas_call(layer_kernel, name='layer', out_shape=(pltpu.VMEM((DP, CAP...  65.2 us
    pallas_call x1, Pallas kernels, on_device(): pl.pallas_call(finish_kernel, name='finish', out_shape=(jax.ShapeDtypeStr...  1.54 us

profile of v4, /device:TPU:96, one launch (start us, length us, event | category | flops | bytes accessed | tf_op | source)
XLA Modules:
  0.0 67.6 jit_solution(6822206664815566862)
XLA Ops:
  0.6 0.0 copy-start
  0.6 65.2 %layer.1 = (bf16[32,32,512]{2,1,0:T(8,128)(2,1)S(1)}, bf16[8,80,128]{2,1,0:T(8,128)(2,1)S(1)}) custom-call(bf16[512,512]{1,0:T(8,128)(2,1)} %ev_any.1, bf16[512,512]{1,0:T(8,128)(2,1)} %go_any.1, bf16[512,2048]{1,0:T(8,128)(2,1)} %w_any.1, bf16[512,512]{1,0:T(8,128)(2,1)} %wo_any.1, s32[1,512]{1,0:T(1,128)} %place.1, s32[1,32]{1,0:T(1,128)} %cnt_any.1, ...), custom_call_target="tpu_custom_call" | custom-call | tf_op jit(solution)/shard_map/layer/pallas_call | solution.py:637
  65.9 0.0 copy-done
  65.9 1.5 %finish.1 = (bf16[512,512]{1,0:T(8,128)(2,1)}, f32[64,512]{1,0:T(8,128)}, f32[16,512]{1,0:T(8,128)}) custom-call(bf16[32,32,512]{2,1,0:T(8,128)(2,1)S(1)} %get-tuple-element.8.ret, bf16[8,80,128]{2,1,0:T(8,128)(2,1)S(1)} %get-tuple-element.9.r4, s32[1,512]{1,0:T(1,128)S(1)} %copy-done), custom_call_target="tpu_custom_call" | custom-call | tf_op jit(solution)/shard_map/finish/pallas_call | solution.py:648
Async XLA Ops:
  0.6 65.2 %copy-start = (s32[1,512]{1,0:T(1,128)S(1)}, s32[1,512]{1,0:T(1,128)}, u32[]{:S(2)}) copy-start(s32[1,512]{1,0:T(1,128)} %place.1) | copy-start | bytes 6148

commit v5 on v4

--- a/solution.py
+++ b/solution.py
@@ -328,6 +328,16 @@
 U, V, Q, K = (slice(128 * i, 128 * i + 128) for i in range(4))
 
 
+SEEN = ((0, 128), (0, 256), (0, 384), (128, 512))
+
+
+def clear_unseen(ref):
+    zero = jnp.zeros((HEADS, 128, 128), BF16)
+    ref[:, 0:128, 128:256] = zero
+    ref[:, 256:384, 384:512] = zero
+    ref[:, 384:512, 0:128] = zero
+
+
 def pair_forward(p, xh, wp, mask, act, slope, wt, gs, att):
     for half in range(2):
         cols = slice(256 * half, 256 * half + 256)
@@ -344,16 +354,19 @@
         for hh in range(2):
             lanes = half_lanes(hh)
             qm = q[rows] * lanes.astype(BF16)
-            half = dot_nt(qm, k[:nk]) * 0.0625
-            th = jnp.tanh(half)
-            silu = half + half * th
-            sig = 0.5 + 0.5 * th
-            grad = (sig + silu * (1.0 - sig)) * 0.125
-            ok = mask[rows, :nk]
-            weights = silu.astype(BF16) * ok
-            wt[2 * p + hh, rows, :nk] = weights
-            gs[2 * p + hh, rows, :nk] = grad.astype(BF16) * ok
-            out = dot(weights, v[:nk]) * lanes
+            scores = dot_nt(qm, k[:nk])
+            for r in range(2):
+                first = 256 * t + 128 * r
+                part, keys = slice(first, first + 128), slice(*SEEN[2 * t + r])
+                half = scores[128 * r : 128 * r + 128, keys] * 0.0625
+                th = jnp.tanh(half)
+                silu = half + half * th
+                sig = 0.5 + 0.5 * th
+                grad = (sig + silu * (1.0 - sig)) * 0.125
+                ok = mask[part, keys]
+                wt[2 * p + hh, part, keys] = silu.astype(BF16) * ok
+                gs[2 * p + hh, part, keys] = grad.astype(BF16) * ok
+            out = dot(wt[2 * p + hh, rows, :nk], v[:nk]) * lanes
             total = out if total is None else total + out
         att[rows, pl.ds(pl.multiple_of(128 * p, 128), 128)] = total
 
@@ -498,20 +511,21 @@
         at, (g, r1, s1, r2, s2, r2x, s2x, r2y, s3x, r5, r3z, rwx, s2w, rwy, s3, r4), sems
     )
     columns = (2, 1, 3, 0)
-    pack(lax.rem(at.x + 2, 4), place, ev, sx)
+    for dxo in columns:
+        pack(lax.rem(at.x + dxo, 4), place, ev, sx)
     small[2].wait()
     pl.semaphore_wait(barrier, DP - 1 + 2 * (REP - 1))
     for dxo in columns:
         counts.start_column(dxo)
-    to_x.start_column(2)
-    for dxo in (1, 3, 0):
-        pack(lax.rem(at.x + dxo, 4), place, ev, sx)
+    for dxo in columns:
         to_x.start_column(dxo)
     small[4].wait()
     for dxo in columns:
         pack(lax.rem(at.x + dxo, 4), place, go, sy)
     small[3].wait()
     allowed_mask(users, mask)
+    clear_unseen(wt)
+    clear_unseen(gs)
     counts.wait()
     for dxo in columns:
         to_y.start_column(dxo)

time: 67.8 us -> 67.9 us (level)
  no operation moved by 1% of the time
where the time goes in v5:
time: 67.9 us; the launch traced here: 67.8 us
  Pallas kernels  66.9 us (99%)
  between operations  0.82 us (1%)
    pallas_call x1, Pallas kernels, on_device(): pl.pallas_call(layer_kernel, name='layer', out_shape=(pltpu.VMEM((DP, CAP...  65.4 us
    pallas_call x1, Pallas kernels, on_device(): pl.pallas_call(finish_kernel, name='finish', out_shape=(jax.ShapeDtypeStr...  1.54 us

profile of v5, /device:TPU:96, one launch (start us, length us, event | category | flops | bytes accessed | tf_op | source)
XLA Modules:
  0.0 67.8 jit_solution(9949161948932651154)
XLA Ops:
  0.6 0.0 copy-start
  0.6 65.4 %layer.1 = (bf16[32,32,512]{2,1,0:T(8,128)(2,1)S(1)}, bf16[8,80,128]{2,1,0:T(8,128)(2,1)S(1)}) custom-call(bf16[512,512]{1,0:T(8,128)(2,1)} %ev_any.1, bf16[512,512]{1,0:T(8,128)(2,1)} %go_any.1, bf16[512,2048]{1,0:T(8,128)(2,1)} %w_any.1, bf16[512,512]{1,0:T(8,128)(2,1)} %wo_any.1, s32[1,512]{1,0:T(1,128)} %place.1, s32[1,32]{1,0:T(1,128)} %cnt_any.1, ...), custom_call_target="tpu_custom_call" | custom-call | tf_op jit(solution)/shard_map/layer/pallas_call | solution.py:651
  66.0 0.0 copy-done
  66.1 1.5 %finish.1 = (bf16[512,512]{1,0:T(8,128)(2,1)}, f32[64,512]{1,0:T(8,128)}, f32[16,512]{1,0:T(8,128)}) custom-call(bf16[32,32,512]{2,1,0:T(8,128)(2,1)S(1)} %get-tuple-element.8.ret, bf16[8,80,128]{2,1,0:T(8,128)(2,1)S(1)} %get-tuple-element.9.r4, s32[1,512]{1,0:T(1,128)S(1)} %copy-done), custom_call_target="tpu_custom_call" | custom-call | tf_op jit(solution)/shard_map/finish/pallas_call | solution.py:662
Async XLA Ops:
  0.6 65.4 %copy-start = (s32[1,512]{1,0:T(1,128)S(1)}, s32[1,512]{1,0:T(1,128)}, u32[]{:S(2)}) copy-start(s32[1,512]{1,0:T(1,128)} %place.1) | copy-start | bytes 6148
